TPU v7x, 512 devices: a whole 4x8x8 slice. The times are simulated.
512 devices in a mesh: lat: 16 (over x_hi, y), lon: 32 (over z, x_lo, core).
Axes of the slice: x: 4 (x_hi: 2, x_lo: 2; x = x_hi * 2 + x_lo), y: 8, z: 8, core: 2. Of those that a mesh axis runs over, the one named last changes fastest.
Arguments:
- height: float32 [1024, 8640], P('lat', 'lon'), may hold values from -6 to 6
- east_flow: float32 [1024, 8640], P('lat', 'lon'), may hold values from -4 to 4
- north_flow: float32 [1024, 8640], P('lat', 'lon'), may hold values from -4 to 4
- legendre: float32 [128, 1024, 2048], P('lon', 'lat'), may hold values from -0.1875 to 0.1875
- love_numbers: float32 [2048], replicated, may hold values from 0.05 to 1
- wavenumbers: int32 [128], replicated, may hold values from 0 to 2047, as said below
- land_sea: int32 [1024, 8640], P('lat', 'lon'), may hold values 0 or 1
Outputs:
- loading: float32 [1024, 8640], P('lat', 'lon')
- surface: float32 [1024, 8640], P('lat', 'lon')
- east_out: float32 [1024, 8640], P('lat', 'lon')
- north_out: float32 [1024, 8640], P('lat', 'lon')
Inputs may be any that keep to these rules, and one draw needn't show every extreme that they name: 128 distinct wavenumbers in no particular order; 0 and 2047 are always among them.
All inputs are finite; a program needn't handle non-finite values. No bound on the sum of `land_sea` on one device may be relied on, other than what follows from the above.
Results may differ from a plain program's by a relative error of at most 0.000078.
Values sent between devices are 32-bit elements; how exact they have to be, the bound alone decides.
A program may use at most 64 MiB of HBM per device.

v0:
```python
import math

import jax
import jax.numpy as jnp
from jax import lax
from jax.sharding import PartitionSpec as P

SUBSTEPS = 4


east_step = 0.3
north_step = 0.3


def extended(block, sides, width, periodic):
    for axis, dim in sides:
        count = lax.axis_size(axis)
        forward = [(i, i + 1) for i in range(count - 1)]
        if periodic:
            forward.append((count - 1, 0))
        backward = [(target, source) for source, target in forward]
        low = lax.ppermute(
            lax.slice_in_dim(block, block.shape[dim] - width, None, axis=dim), axis, forward
        )
        high = lax.ppermute(lax.slice_in_dim(block, 0, width, axis=dim), axis, backward)
        block = jnp.concatenate([low, block, high], axis=dim)
    return block


def harmonic_rows(wavenumbers, first_column, column_count, period):
    columns = first_column + jnp.arange(column_count, dtype=jnp.int32)
    product = wavenumbers[:, None] * columns[None, :] % period
    angles = 2.0 * math.pi / period * product.astype(jnp.float32)
    stacked = jnp.stack([jnp.cos(angles), jnp.sin(angles)], axis=1)
    return stacked.reshape(2 * wavenumbers.shape[0], column_count)


def band_rim(field):
    return extended(field, (("lat", 0),), 1, False)


def sector_rim(field):
    return extended(field, (("lon", 1),), 1, True)


def shards(height, east_flow, north_flow, legendre, love_numbers, wavenumbers, land_sea):
    highest = lax.Precision.HIGHEST
    band_rows, sector_cols = height.shape
    all_cols = sector_cols * lax.axis_size("lon")
    all_waves = wavenumbers.shape[0]
    own_waves = legendre.shape[0]
    sector_index = lax.axis_index("lon")
    harmonics = harmonic_rows(wavenumbers, sector_index * sector_cols, sector_cols, all_cols)
    forward_scale = 1.0 / math.sqrt(all_cols)
    partial_rows = forward_scale * lax.dot_general(
        harmonics, height, (((1,), (1,)), ((), ())), precision=highest
    )
    totals = lax.psum(partial_rows, "lon")
    owned = lax.dynamic_slice_in_dim(totals, sector_index * (2 * own_waves), 2 * own_waves, 0)
    owned = owned.reshape(own_waves, 2, band_rows)
    partial_value = jnp.einsum("mtl,mpt->mpl", legendre, owned, precision=highest)
    spectral = lax.psum(partial_value, "lat") * love_numbers[None, None, :]
    synthesized = jnp.einsum("mtl,mpl->mpt", legendre, spectral, precision=highest).reshape(
        2 * own_waves, band_rows
    )
    back_scale = 1.0 / math.sqrt(all_waves)
    loading = (
        lax.dot_general(
            lax.all_gather(synthesized, "lon", axis=0, tiled=True),
            harmonics,
            (((0,), (0,)), ((), ())),
            precision=highest,
        )
        * back_scale
    )
    wet_cells = land_sea.astype(jnp.float32)
    surface = height
    east_out = east_flow
    north_out = north_flow
    for substep in range(SUBSTEPS):
        pressure = surface - loading
        pressure_lat = band_rim(pressure)
        pressure_lon = sector_rim(pressure)
        east_out = wet_cells * (east_out - east_step * (pressure_lon[:, 2:] - pressure_lon[:, :-2]))
        north_out = wet_cells * (north_out - north_step * (pressure_lat[2:] - pressure_lat[:-2]))
        east_wide = sector_rim(east_out)
        north_wide = band_rim(north_out)
        change = east_step * (east_wide[:, 2:] - east_wide[:, :-2]) + north_step * (
            north_wide[2:] - north_wide[:-2]
        )
        surface = surface - wet_cells * change
    return (loading, surface, east_out, north_out)


def solution(mesh):
    return jax.shard_map(
        shards,
        mesh=mesh,
        in_specs=(
            P("lat", "lon"),
            P("lat", "lon"),
            P("lat", "lon"),
            P("lon", "lat", None),
            P(),
            P(),
            P("lat", "lon"),
        ),
        out_specs=(P("lat", "lon"), P("lat", "lon"), P("lat", "lon"), P("lat", "lon")),
        check_vma=False,
    )
```

profile of v0, /device:TPU:56, one launch (start us, length us, event | category | flops | bytes accessed | tf_op | source)
XLA Modules:
  0.0 582.8 jit_solution(6953861917037026702)
XLA Ops:
  7.2 7.9 %fusion.62 = (f32[128,1,270]{2,1,0:T(1,128)S(1)}, f32[128,1,270]{2,1,0:T(1,128)S(1)}) fusion(s32[270]{0:T(512)S(1)} %iota_add_fusion, s32[128]{0:T(128)} %param.12), kind=kLoop, calls=%fused_computation.98 | loop fusion | flops 311040 | bytes 278072 | tf_op jit(solution)/shard_map/cos | solution.py:34
  15.9 2.0 convolution_multiply_fusion
  18.0 215.3 %all-reduce.3.cloned.1.call-done = f32[256,64]{1,0:T(8,128)} async-done(((f32[256,64]{1,0:T(8,128)}), f32[256,64]{1,0:T(8,128)}) %all-reduce.3.cloned.1.call-update) | async-done | bytes 65552 | tf_op jit(solution)/shard_map/psum | solution.py:58
  233.9 1.7 fusion.86
  235.7 149.2 %all-reduce.5.cloned.1.call-done = f32[4,2,2048]{2,1,0:T(2,128)} async-done(((f32[4,2,2048]{2,1,0:T(2,128)}), f32[4,2,2048]{2,1,0:T(2,128)}) %all-reduce.5.cloned.1.call-update) | async-done | bytes 65552 | tf_op jit(solution)/shard_map/psum | solution.py:62
  384.8 2.7 fusion.58
  387.5 35.5 %all_gather.3 = f32[256,64]{1,0:T(8,128)S(1)} all-gather(f32[8,64]{1,0:T(8,128)S(1)} %bitcast.9), channel_id=1, replica_groups=mesh['lat'=16,'lon'=32] {'lon'}, dimensions={0}, use_global_device_ids=true | all-gather | bytes 67584 | tf_op jit(solution)/shard_map/all_gather | solution.py:69
  423.5 1.9 collective-permute-start.4
  425.4 7.5 %collective-permute-start.5 = (f32[1,270]{1,0:T(1,128)S(1)}, f32[1,270]{1,0:T(1,128)S(1)}, u32[]{:S(2)}, u32[]{:S(2)}) collective-permute-start(f32[1,270]{1,0:T(1,128)S(1)} %get-tuple-element.49), channel_id=1, source_target_pairs={{0,32},{32,64},{64,96},{96,128},{128,160},{160,192},{192,224},{224... | collective-permute-start | bytes 3248 | tf_op jit(solution)/shard_map/ppermute | solution.py:22
  433.0 1.9 collective-permute-start
  435.0 2.4 collective-permute-start.1
  437.4 4.9 collective-permute-done.1
  442.5 1.9 collective-permute-start.6
  444.4 7.5 %collective-permute-start.7 = (f32[1,270]{1,0:T(1,128)S(1)}, f32[1,270]{1,0:T(1,128)S(1)}, u32[]{:S(2)}, u32[]{:S(2)}) collective-permute-start(f32[1,270]{1,0:T(1,128)S(1)} %get-tuple-element.47), channel_id=1, source_target_pairs={{0,32},{32,64},{64,96},{96,128},{128,160},{160,192},{192,224},{224... | collective-permute-start | bytes 3248 | tf_op jit(solution)/shard_map/ppermute | solution.py:22
  452.0 1.9 collective-permute-start.2
  454.0 2.4 collective-permute-start.3
  456.4 4.9 collective-permute-done.3
  461.5 1.9 collective-permute-start.12
  463.4 7.5 %collective-permute-start.13 = (f32[1,270]{1,0:T(1,128)S(1)}, f32[1,270]{1,0:T(1,128)S(1)}, u32[]{:S(2)}, u32[]{:S(2)}) collective-permute-start(f32[1,270]{1,0:T(1,128)S(1)} %get-tuple-element.41), channel_id=1, source_target_pairs={{0,32},{32,64},{64,96},{96,128},{128,160},{160,192},{192,224},{224... | collective-permute-start | bytes 3248 | tf_op jit(solution)/shard_map/ppermute | solution.py:22
  471.0 1.9 collective-permute-start.8
  472.9 2.4 collective-permute-start.9
  475.4 4.9 collective-permute-done.9
  480.4 1.9 collective-permute-start.14
  482.4 7.5 %collective-permute-start.15 = (f32[1,270]{1,0:T(1,128)S(1)}, f32[1,270]{1,0:T(1,128)S(1)}, u32[]{:S(2)}, u32[]{:S(2)}) collective-permute-start(f32[1,270]{1,0:T(1,128)S(1)} %get-tuple-element.39), channel_id=1, source_target_pairs={{0,32},{32,64},{64,96},{96,128},{128,160},{160,192},{192,224},{224... | collective-permute-start | bytes 3248 | tf_op jit(solution)/shard_map/ppermute | solution.py:22
  490.0 1.9 collective-permute-start.10
  491.9 2.4 collective-permute-start.11
  494.3 4.9 collective-permute-done.11
  499.4 1.9 collective-permute-start.20
  501.3 7.5 %collective-permute-start.21 = (f32[1,270]{1,0:T(1,128)S(1)}, f32[1,270]{1,0:T(1,128)S(1)}, u32[]{:S(2)}, u32[]{:S(2)}) collective-permute-start(f32[1,270]{1,0:T(1,128)S(1)} %get-tuple-element.33), channel_id=1, source_target_pairs={{0,32},{32,64},{64,96},{96,128},{128,160},{160,192},{192,224},{224... | collective-permute-start | bytes 3248 | tf_op jit(solution)/shard_map/ppermute | solution.py:22
  509.0 1.9 collective-permute-start.16
  510.9 2.4 collective-permute-start.17
  513.3 4.9 collective-permute-done.17
  518.4 1.9 collective-permute-start.22
  520.3 7.5 %collective-permute-start.23 = (f32[1,270]{1,0:T(1,128)S(1)}, f32[1,270]{1,0:T(1,128)S(1)}, u32[]{:S(2)}, u32[]{:S(2)}) collective-permute-start(f32[1,270]{1,0:T(1,128)S(1)} %get-tuple-element.31), channel_id=1, source_target_pairs={{0,32},{32,64},{64,96},{96,128},{128,160},{160,192},{192,224},{224... | collective-permute-start | bytes 3248 | tf_op jit(solution)/shard_map/ppermute | solution.py:22
  527.9 1.9 collective-permute-start.18
  529.9 2.4 collective-permute-start.19
  532.3 4.9 collective-permute-done.19
  537.4 1.9 collective-permute-start.28
  539.3 7.5 %collective-permute-start.29 = (f32[1,270]{1,0:T(1,128)S(1)}, f32[1,270]{1,0:T(1,128)S(1)}, u32[]{:S(2)}, u32[]{:S(2)}) collective-permute-start(f32[1,270]{1,0:T(1,128)S(1)} %get-tuple-element.25), channel_id=1, source_target_pairs={{0,32},{32,64},{64,96},{96,128},{128,160},{160,192},{192,224},{224... | collective-permute-start | bytes 3248 | tf_op jit(solution)/shard_map/ppermute | solution.py:22
  546.9 1.9 collective-permute-start.24
  548.8 2.4 collective-permute-start.25
  551.3 4.9 collective-permute-done.25
  556.4 1.9 collective-permute-start.30
  558.3 7.5 %collective-permute-start.31 = (f32[1,270]{1,0:T(1,128)S(1)}, f32[1,270]{1,0:T(1,128)S(1)}, u32[]{:S(2)}, u32[]{:S(2)}) collective-permute-start(f32[1,270]{1,0:T(1,128)S(1)} %get-tuple-element.23), channel_id=1, source_target_pairs={{0,32},{32,64},{64,96},{96,128},{128,160},{160,192},{192,224},{224... | collective-permute-start | bytes 3248 | tf_op jit(solution)/shard_map/ppermute | solution.py:22
  565.9 1.9 collective-permute-start.26
  567.8 2.4 collective-permute-start.27
  570.3 4.9 collective-permute-done.27
  575.2 0.8 fusion.6
  (74 shorter events, 3.6 us)
Async XLA Ops:
  7.2 226.8 %copy-start = (f32[4,64,2048]{2,1,0:T(8,128)S(1)}, f32[4,64,2048]{2,1,0:T(8,128)}, u32[]{:S(2)}) copy-start(f32[4,64,2048]{2,1,0:T(8,128)} %param.10) | copy-start | bytes 6291460
  7.2 226.1 %all-reduce.3.cloned.1.call-start = ((), (), s32[]{:S(2)}) async-start(), calls=%async_computation | async-start | bytes 262144 | tf_op jit(solution)/shard_map/psum | solution.py:58
  15.2 369.7 %copy-start.8 = (f32[2048]{0:T(1024)S(1)}, f32[2048]{0:T(1024)}, u32[]{:S(2)}) copy-start(f32[2048]{0:T(1024)} %param.11) | copy-start | bytes 24580
  17.9 366.9 %all-reduce.5.cloned.1.call-start = ((), (), s32[]{:S(2)}) async-start(), calls=%async_computation.1 | async-start | bytes 131072 | tf_op jit(solution)/shard_map/psum | solution.py:62
  233.9 189.1 %copy-start.3 = (f32[64,270]{1,0:T(8,128)S(1)}, f32[64,270]{1,0:T(8,128)}, u32[]{:S(2)}) copy-start(f32[64,270]{1,0:T(8,128)} %param.7) | copy-start | bytes 207364
  235.7 206.7 %copy-start.1 = (s32[64,270]{1,0:T(8,128)S(1)}, s32[64,270]{1,0:T(8,128)}, u32[]{:S(2)}) copy-start(s32[64,270]{1,0:T(8,128)} %param.13) | copy-start | bytes 207364
  235.7 206.7 %copy-start.6 = (f32[64,270]{1,0:T(8,128)S(1)}, f32[64,270]{1,0:T(8,128)}, u32[]{:S(2)}) copy-start(f32[64,270]{1,0:T(8,128)} %param.8) | copy-start | bytes 207364
  235.7 206.7 %copy-start.7 = (f32[64,270]{1,0:T(8,128)S(1)}, f32[64,270]{1,0:T(8,128)}, u32[]{:S(2)}) copy-start(f32[64,270]{1,0:T(8,128)} %param.9) | copy-start | bytes 207364
  423.5 113.7 %copy-start.2 = (f32[64,270]{1,0:T(8,128)}, f32[64,270]{1,0:T(8,128)S(1)}, u32[]{:S(2)}) copy-start(f32[64,270]{1,0:T(8,128)S(1)} %get-tuple-element.53) | copy-start | bytes 207364
  423.5 18.8 %collective-permute-start.4 = (f32[1,270]{1,0:T(1,128)S(1)}, f32[1,270]{1,0:T(1,128)S(1)}, u32[]{:S(2)}, u32[]{:S(2)}) collective-permute-start(f32[1,270]{1,0:T(1,128)S(1)} %get-tuple-element.48), channel_id=1, source_target_pairs={{32,0},{64,32},{96,64},{128,96},{160,128},{192,160},{224,192},{256... | collective-permute-start | bytes 3248 | tf_op jit(solution)/shard_map/ppermute | solution.py:25
  425.4 16.9 %collective-permute-start.5 = (f32[1,270]{1,0:T(1,128)S(1)}, f32[1,270]{1,0:T(1,128)S(1)}, u32[]{:S(2)}, u32[]{:S(2)}) collective-permute-start(f32[1,270]{1,0:T(1,128)S(1)} %get-tuple-element.49), channel_id=1, source_target_pairs={{0,32},{32,64},{64,96},{96,128},{128,160},{160,192},{192,224},{224... | collective-permute-start | bytes 3248 | tf_op jit(solution)/shard_map/ppermute | solution.py:22
  433.0 4.3 collective-permute-start
  435.0 7.3 %collective-permute-start.1 = (f32[64,1]{1,0:T(8,128)S(1)}, f32[64,1]{1,0:T(8,128)S(1)}, u32[]{:S(2)}, u32[]{:S(2)}) collective-permute-start(f32[64,1]{1,0:T(8,128)S(1)} %get-tuple-element.45), channel_id=1, source_target_pairs={{0,1},{1,2},{2,3},{3,4},{4,5},{5,6},{6,7},{7,8},{8,9},{9,10},{10,1... | collective-permute-start | bytes 776 | tf_op jit(solution)/shard_map/ppermute | solution.py:22
  442.5 18.8 %collective-permute-start.6 = (f32[1,270]{1,0:T(1,128)S(1)}, f32[1,270]{1,0:T(1,128)S(1)}, u32[]{:S(2)}, u32[]{:S(2)}) collective-permute-start(f32[1,270]{1,0:T(1,128)S(1)} %get-tuple-element.46), channel_id=1, source_target_pairs={{32,0},{64,32},{96,64},{128,96},{160,128},{192,160},{224,192},{256... | collective-permute-start | bytes 3248 | tf_op jit(solution)/shard_map/ppermute | solution.py:25
  444.4 16.9 %collective-permute-start.7 = (f32[1,270]{1,0:T(1,128)S(1)}, f32[1,270]{1,0:T(1,128)S(1)}, u32[]{:S(2)}, u32[]{:S(2)}) collective-permute-start(f32[1,270]{1,0:T(1,128)S(1)} %get-tuple-element.47), channel_id=1, source_target_pairs={{0,32},{32,64},{64,96},{96,128},{128,160},{160,192},{192,224},{224... | collective-permute-start | bytes 3248 | tf_op jit(solution)/shard_map/ppermute | solution.py:22
  452.0 4.3 collective-permute-start.2
  454.0 7.3 %collective-permute-start.3 = (f32[64,1]{1,0:T(8,128)S(1)}, f32[64,1]{1,0:T(8,128)S(1)}, u32[]{:S(2)}, u32[]{:S(2)}) collective-permute-start(f32[64,1]{1,0:T(8,128)S(1)} %get-tuple-element.43), channel_id=1, source_target_pairs={{0,1},{1,2},{2,3},{3,4},{4,5},{5,6},{6,7},{7,8},{8,9},{9,10},{10,1... | collective-permute-start | bytes 776 | tf_op jit(solution)/shard_map/ppermute | solution.py:22
  461.5 18.8 %collective-permute-start.12 = (f32[1,270]{1,0:T(1,128)S(1)}, f32[1,270]{1,0:T(1,128)S(1)}, u32[]{:S(2)}, u32[]{:S(2)}) collective-permute-start(f32[1,270]{1,0:T(1,128)S(1)} %get-tuple-element.40), channel_id=1, source_target_pairs={{32,0},{64,32},{96,64},{128,96},{160,128},{192,160},{224,192},{256... | collective-permute-start | bytes 3248 | tf_op jit(solution)/shard_map/ppermute | solution.py:25
  463.4 16.9 %collective-permute-start.13 = (f32[1,270]{1,0:T(1,128)S(1)}, f32[1,270]{1,0:T(1,128)S(1)}, u32[]{:S(2)}, u32[]{:S(2)}) collective-permute-start(f32[1,270]{1,0:T(1,128)S(1)} %get-tuple-element.41), channel_id=1, source_target_pairs={{0,32},{32,64},{64,96},{96,128},{128,160},{160,192},{192,224},{224... | collective-permute-start | bytes 3248 | tf_op jit(solution)/shard_map/ppermute | solution.py:22
  471.0 4.3 collective-permute-start.8
  472.9 7.3 %collective-permute-start.9 = (f32[64,1]{1,0:T(8,128)S(1)}, f32[64,1]{1,0:T(8,128)S(1)}, u32[]{:S(2)}, u32[]{:S(2)}) collective-permute-start(f32[64,1]{1,0:T(8,128)S(1)} %get-tuple-element.37), channel_id=1, source_target_pairs={{0,1},{1,2},{2,3},{3,4},{4,5},{5,6},{6,7},{7,8},{8,9},{9,10},{10,1... | collective-permute-start | bytes 776 | tf_op jit(solution)/shard_map/ppermute | solution.py:22
  480.4 18.8 %collective-permute-start.14 = (f32[1,270]{1,0:T(1,128)S(1)}, f32[1,270]{1,0:T(1,128)S(1)}, u32[]{:S(2)}, u32[]{:S(2)}) collective-permute-start(f32[1,270]{1,0:T(1,128)S(1)} %get-tuple-element.38), channel_id=1, source_target_pairs={{32,0},{64,32},{96,64},{128,96},{160,128},{192,160},{224,192},{256... | collective-permute-start | bytes 3248 | tf_op jit(solution)/shard_map/ppermute | solution.py:25
  482.4 16.9 %collective-permute-start.15 = (f32[1,270]{1,0:T(1,128)S(1)}, f32[1,270]{1,0:T(1,128)S(1)}, u32[]{:S(2)}, u32[]{:S(2)}) collective-permute-start(f32[1,270]{1,0:T(1,128)S(1)} %get-tuple-element.39), channel_id=1, source_target_pairs={{0,32},{32,64},{64,96},{96,128},{128,160},{160,192},{192,224},{224... | collective-permute-start | bytes 3248 | tf_op jit(solution)/shard_map/ppermute | solution.py:22
  490.0 4.3 collective-permute-start.10
  491.9 7.3 %collective-permute-start.11 = (f32[64,1]{1,0:T(8,128)S(1)}, f32[64,1]{1,0:T(8,128)S(1)}, u32[]{:S(2)}, u32[]{:S(2)}) collective-permute-start(f32[64,1]{1,0:T(8,128)S(1)} %get-tuple-element.35), channel_id=1, source_target_pairs={{0,1},{1,2},{2,3},{3,4},{4,5},{5,6},{6,7},{7,8},{8,9},{9,10},{10,1... | collective-permute-start | bytes 776 | tf_op jit(solution)/shard_map/ppermute | solution.py:22
  499.4 18.8 %collective-permute-start.20 = (f32[1,270]{1,0:T(1,128)S(1)}, f32[1,270]{1,0:T(1,128)S(1)}, u32[]{:S(2)}, u32[]{:S(2)}) collective-permute-start(f32[1,270]{1,0:T(1,128)S(1)} %get-tuple-element.32), channel_id=1, source_target_pairs={{32,0},{64,32},{96,64},{128,96},{160,128},{192,160},{224,192},{256... | collective-permute-start | bytes 3248 | tf_op jit(solution)/shard_map/ppermute | solution.py:25
  501.3 16.9 %collective-permute-start.21 = (f32[1,270]{1,0:T(1,128)S(1)}, f32[1,270]{1,0:T(1,128)S(1)}, u32[]{:S(2)}, u32[]{:S(2)}) collective-permute-start(f32[1,270]{1,0:T(1,128)S(1)} %get-tuple-element.33), channel_id=1, source_target_pairs={{0,32},{32,64},{64,96},{96,128},{128,160},{160,192},{192,224},{224... | collective-permute-start | bytes 3248 | tf_op jit(solution)/shard_map/ppermute | solution.py:22
  509.0 4.3 collective-permute-start.16
  510.9 7.3 %collective-permute-start.17 = (f32[64,1]{1,0:T(8,128)S(1)}, f32[64,1]{1,0:T(8,128)S(1)}, u32[]{:S(2)}, u32[]{:S(2)}) collective-permute-start(f32[64,1]{1,0:T(8,128)S(1)} %get-tuple-element.29), channel_id=1, source_target_pairs={{0,1},{1,2},{2,3},{3,4},{4,5},{5,6},{6,7},{7,8},{8,9},{9,10},{10,1... | collective-permute-start | bytes 776 | tf_op jit(solution)/shard_map/ppermute | solution.py:22
  518.4 18.8 %collective-permute-start.22 = (f32[1,270]{1,0:T(1,128)S(1)}, f32[1,270]{1,0:T(1,128)S(1)}, u32[]{:S(2)}, u32[]{:S(2)}) collective-permute-start(f32[1,270]{1,0:T(1,128)S(1)} %get-tuple-element.30), channel_id=1, source_target_pairs={{32,0},{64,32},{96,64},{128,96},{160,128},{192,160},{224,192},{256... | collective-permute-start | bytes 3248 | tf_op jit(solution)/shard_map/ppermute | solution.py:25
  520.3 16.9 %collective-permute-start.23 = (f32[1,270]{1,0:T(1,128)S(1)}, f32[1,270]{1,0:T(1,128)S(1)}, u32[]{:S(2)}, u32[]{:S(2)}) collective-permute-start(f32[1,270]{1,0:T(1,128)S(1)} %get-tuple-element.31), channel_id=1, source_target_pairs={{0,32},{32,64},{64,96},{96,128},{128,160},{160,192},{192,224},{224... | collective-permute-start | bytes 3248 | tf_op jit(solution)/shard_map/ppermute | solution.py:22
  527.9 4.3 collective-permute-start.18
  529.9 7.3 %collective-permute-start.19 = (f32[64,1]{1,0:T(8,128)S(1)}, f32[64,1]{1,0:T(8,128)S(1)}, u32[]{:S(2)}, u32[]{:S(2)}) collective-permute-start(f32[64,1]{1,0:T(8,128)S(1)} %get-tuple-element.27), channel_id=1, source_target_pairs={{0,1},{1,2},{2,3},{3,4},{4,5},{5,6},{6,7},{7,8},{8,9},{9,10},{10,1... | collective-permute-start | bytes 776 | tf_op jit(solution)/shard_map/ppermute | solution.py:22
  537.4 18.8 %collective-permute-start.28 = (f32[1,270]{1,0:T(1,128)S(1)}, f32[1,270]{1,0:T(1,128)S(1)}, u32[]{:S(2)}, u32[]{:S(2)}) collective-permute-start(f32[1,270]{1,0:T(1,128)S(1)} %get-tuple-element.24), channel_id=1, source_target_pairs={{32,0},{64,32},{96,64},{128,96},{160,128},{192,160},{224,192},{256... | collective-permute-start | bytes 3248 | tf_op jit(solution)/shard_map/ppermute | solution.py:25
  539.3 16.9 %collective-permute-start.29 = (f32[1,270]{1,0:T(1,128)S(1)}, f32[1,270]{1,0:T(1,128)S(1)}, u32[]{:S(2)}, u32[]{:S(2)}) collective-permute-start(f32[1,270]{1,0:T(1,128)S(1)} %get-tuple-element.25), channel_id=1, source_target_pairs={{0,32},{32,64},{64,96},{96,128},{128,160},{160,192},{192,224},{224... | collective-permute-start | bytes 3248 | tf_op jit(solution)/shard_map/ppermute | solution.py:22
  546.9 4.3 collective-permute-start.24
  548.8 7.3 %collective-permute-start.25 = (f32[64,1]{1,0:T(8,128)S(1)}, f32[64,1]{1,0:T(8,128)S(1)}, u32[]{:S(2)}, u32[]{:S(2)}) collective-permute-start(f32[64,1]{1,0:T(8,128)S(1)} %get-tuple-element.21), channel_id=1, source_target_pairs={{0,1},{1,2},{2,3},{3,4},{4,5},{5,6},{6,7},{7,8},{8,9},{9,10},{10,1... | collective-permute-start | bytes 776 | tf_op jit(solution)/shard_map/ppermute | solution.py:22
  556.3 19.6 %copy-start.4 = (f32[64,270]{1,0:T(8,128)}, f32[64,270]{1,0:T(8,128)S(1)}, u32[]{:S(2)}) copy-start(f32[64,270]{1,0:T(8,128)S(1)} %get-tuple-element.10) | copy-start | bytes 207364
  556.3 19.6 %copy-start.5 = (f32[64,270]{1,0:T(8,128)}, f32[64,270]{1,0:T(8,128)S(1)}, u32[]{:S(2)}) copy-start(f32[64,270]{1,0:T(8,128)S(1)} %get-tuple-element.11) | copy-start | bytes 207364
  556.4 18.8 %collective-permute-start.30 = (f32[1,270]{1,0:T(1,128)S(1)}, f32[1,270]{1,0:T(1,128)S(1)}, u32[]{:S(2)}, u32[]{:S(2)}) collective-permute-start(f32[1,270]{1,0:T(1,128)S(1)} %get-tuple-element.22), channel_id=1, source_target_pairs={{32,0},{64,32},{96,64},{128,96},{160,128},{192,160},{224,192},{256... | collective-permute-start | bytes 3248 | tf_op jit(solution)/shard_map/ppermute | solution.py:25
  558.3 16.9 %collective-permute-start.31 = (f32[1,270]{1,0:T(1,128)S(1)}, f32[1,270]{1,0:T(1,128)S(1)}, u32[]{:S(2)}, u32[]{:S(2)}) collective-permute-start(f32[1,270]{1,0:T(1,128)S(1)} %get-tuple-element.23), channel_id=1, source_target_pairs={{0,32},{32,64},{64,96},{96,128},{128,160},{160,192},{192,224},{224... | collective-permute-start | bytes 3248 | tf_op jit(solution)/shard_map/ppermute | solution.py:22
  565.9 4.3 collective-permute-start.26
  567.8 7.3 %collective-permute-start.27 = (f32[64,1]{1,0:T(8,128)S(1)}, f32[64,1]{1,0:T(8,128)S(1)}, u32[]{:S(2)}, u32[]{:S(2)}) collective-permute-start(f32[64,1]{1,0:T(8,128)S(1)} %get-tuple-element.19), channel_id=1, source_target_pairs={{0,1},{1,2},{2,3},{3,4},{4,5},{5,6},{6,7},{7,8},{8,9},{9,10},{10,1... | collective-permute-start | bytes 776 | tf_op jit(solution)/shard_map/ppermute | solution.py:22
Sparse Core Ops, SparseCore 0:
  18.0 215.1 all-reduce.2
  236.7 148.0 all-reduce.4
where the time goes:
time: 584 us; the launch traced here: 583 us
  waiting for transfers between devices  404 us (69%)
  starting transfers between devices  110 us (19%)
  blocking collectives  35.5 us (6%)
  between operations  14.6 us (2%)
  other arithmetic  10 us (2%)
  matrix products  6.82 us (1%)
    psum x1, waiting for transfers between devices, shards(): totals = lax.psum(partial_rows, 'lon')  215 us
    psum x1, waiting for transfers between devices, shards(): spectral = lax.psum(partial_value, 'lat') * love_numbers[None, None, :]  149 us
    ppermute x16, starting transfers between devices, extended(): lax.ppermute(lax.slice_in_dim(block, block.shape[dim] - width, None, axis...  79.5 us
    ppermute x16, waiting for transfers between devices, extended(): lax.ppermute(lax.slice_in_dim(block, block.shape[dim] - width, None, axis...  39.4 us
    all_gather x1, blocking collectives, shards(): lax.all_gather(synthesized, 'lon', axis=0, tiled=True)  35.5 us
    ppermute x16, starting transfers between devices, extended(): lax.ppermute(lax.slice_in_dim(block, 0, width, axis=dim), axis, backward)  30.7 us
  transfers between devices with their start and end apart: 34, of which 10 were waited for; matrix products, arithmetic and copies ran while one was open for 0% of the time, Pallas kernels for 0%

commit v1 on v0

v1 whole, which is shorter than its diff:
```python
import functools
import math

import jax
import jax.numpy as jnp
from jax import lax
from jax.experimental import pallas as pl
from jax.experimental.pallas import tpu as pltpu
from jax.sharding import PartitionSpec as P

SUBSTEPS = 4
HALO = 2 * SUBSTEPS
LANES = 128
EAST_STEP = 0.3
NORTH_STEP = 0.3
MESH = pl.DeviceIdType.MESH
HIGHEST = lax.Precision.HIGHEST


def dot(a, b, dims):
    return lax.dot_general(
        a, b, (dims, ((), ())), precision=HIGHEST, preferred_element_type=jnp.float32
    )


def ring_order(n):
    return sorted(range(n), key=lambda d: -min(d, n - d))


def lat_partners(n_lat, lat):
    n_y = min(8, n_lat)
    x_hi, y = lat // n_y, lat % n_y
    steps = [(dx, dy) for dx in range(n_lat // n_y) for dy in range(n_y) if dx or dy]
    steps.sort(key=lambda s: -(2 * s[0] + min(s[1], n_y - s[1])))
    n_x = n_lat // n_y
    return [((x_hi + dx) % n_x) * n_y + (y + dy) % n_y for dx, dy in steps]


def lon_partners(n_lon, lon):
    n_z = n_lon // 4
    z, low = lon // 4, lon % 4
    steps = [(dz, e) for dz in ring_order(n_z) for e in (2, 3, 1, 0) if dz or e]
    return [((z + dz) % n_z) * 4 + (low + e) % 4 for dz, e in steps]


def kernel(
    n_lat,
    n_lon,
    height_ref,
    east_ref,
    north_ref,
    land_ref,
    legendre_ref,
    love_ref,
    waves_ref,
    loading_out,
    surface_out,
    east_out_ref,
    north_out_ref,
    fields,
    harmonics,
    twice,
    leg_own,
    leg_halo,
    a_out,
    a_in,
    b_out,
    b_in,
    c_out,
    c_in,
    d_out,
    d_in,
    to_left,
    to_right,
    from_right,
    from_left,
    leg_sem,
    send_sem,
    recv_sem,
    edge_send,
    edge_recv,
):
    lat = lax.axis_index("lat")
    lon = lax.axis_index("lon")
    rows, cols = height_ref.shape
    own = legendre_ref.shape[0]
    width = fields.shape[2]
    period = cols * n_lon
    base, rest = cols // LANES * LANES, cols % LANES
    lats = lat_partners(n_lat, lat)
    lons = lon_partners(n_lon, lon)

    barrier = pltpu.get_barrier_semaphore()
    for other in lons:
        pl.semaphore_signal(barrier, inc=1, device_id=(lat, other), device_id_type=MESH)
    for other in lats:
        pl.semaphore_signal(barrier, inc=1, device_id=(other, lon), device_id_type=MESH)
    leg_copy = pltpu.make_async_copy(legendre_ref, leg_own, leg_sem)
    leg_copy.start()

    for f, ref in enumerate((height_ref, east_ref, north_ref, land_ref)):
        fields[f, 0:rows, base:width] = jnp.zeros((rows, width - base), jnp.float32)
        fields[f, 0:rows, 0:cols] = ref[...].astype(jnp.float32)
    twice[0:rows, :] = fields[0, 0:rows, :]
    twice[rows : 2 * rows, :] = fields[0, 0:rows, :]

    count = waves_ref.shape[1]
    waves = jnp.broadcast_to(waves_ref[...].astype(jnp.float32), (LANES, count)).T
    start = jnp.bitwise_and(waves.astype(jnp.int32) * lon, n_lon - 1).astype(jnp.float32) * cols
    quarter = period // 4
    lane = lax.broadcasted_iota(jnp.int32, (8, width), 1)
    column = jnp.where(lane < width - 64, lane, lane - width).astype(jnp.float32)
    upper = lax.broadcasted_iota(jnp.int32, (8, width), 0) < 4
    for g in range(count // 8):
        wave = jnp.concatenate([waves[8 * g : 8 * g + 8]] * (width // LANES), axis=1)
        first = jnp.concatenate([start[8 * g : 8 * g + 8]] * (width // LANES), axis=1)
        r = wave * column + first
        turn = (r * (1.0 / quarter) + 4096.5).astype(jnp.int32)
        d = r - (turn - 4096).astype(jnp.float32) * quarter
        phi = d * (2.0 * math.pi / period)
        s = phi * phi
        sin = 1.0 / 362880.0
        sin = sin * s - 1.0 / 5040.0
        sin = sin * s + 1.0 / 120.0
        sin = sin * s - 1.0 / 6.0
        sin = phi + phi * (s * sin)
        cos = -1.0 / 3628800.0
        cos = cos * s + 1.0 / 40320.0
        cos = cos * s - 1.0 / 720.0
        cos = cos * s + 1.0 / 24.0
        cos = cos * s - 0.5
        cos = 1.0 + s * cos
        odd = jnp.bitwise_and(turn, 1) == 1
        cos_minus = jnp.bitwise_and(turn + 1, 2) == 2
        sin_minus = jnp.bitwise_and(turn, 2) == 2
        c = jnp.where(odd, sin, cos)
        c = jnp.where(cos_minus, -c, c)
        n = jnp.where(odd, cos, sin)
        n = jnp.where(sin_minus, -n, n)
        harmonics[16 * g : 16 * g + 8, :] = jnp.where(upper, c, pltpu.roll(n, 4, 0))
        harmonics[16 * g + 8 : 16 * g + 16, :] = jnp.where(upper, pltpu.roll(c, 4, 0), n)

    partial = dot(harmonics[...], twice[...], ((1,), (1,))) * (1.0 / math.sqrt(period))
    half = lax.broadcasted_iota(jnp.int32, (8, LANES), 1) < rows
    for j in range(n_lon):
        block = partial[8 * j : 8 * j + 8]
        a_out[j] = jnp.where(half, block, pltpu.roll(block, 4, 0))[0:4]

    pl.semaphore_wait(barrier, n_lat + n_lon - 2)

    def lon_copy(k, src, dst, other):
        return pltpu.make_async_remote_copy(
            src_ref=src,
            dst_ref=dst,
            send_sem=send_sem.at[k],
            recv_sem=recv_sem.at[k],
            device_id=(lat, other),
            device_id_type=MESH,
        )

    def lat_copy(k, src, dst, other):
        return pltpu.make_async_remote_copy(
            src_ref=src,
            dst_ref=dst,
            send_sem=send_sem.at[k],
            recv_sem=recv_sem.at[k],
            device_id=(other, lon),
            device_id_type=MESH,
        )

    def all_received(k, ref, n):
        pltpu.make_async_copy(ref.at[pl.ds(0, n)], ref.at[pl.ds(0, n)], recv_sem.at[k]).wait()

    def all_sent(k, ref, n):
        pltpu.make_async_copy(ref.at[pl.ds(0, n)], ref.at[pl.ds(0, n)], send_sem.at[k]).wait()

    for other in lons:
        lon_copy(0, a_out.at[other], a_in.at[lon], other).start()
    a_in[lon] = a_out[lon]

    below, above = jnp.minimum(lat + 1, n_lat - 1), jnp.maximum(lat - 1, 0)

    def edge_copy(k, src, dst, where):
        return pltpu.make_async_remote_copy(
            src_ref=src,
            dst_ref=dst,
            send_sem=edge_send.at[k],
            recv_sem=edge_recv.at[k],
            device_id=where,
            device_id_type=MESH,
        )

    low_rows = edge_copy(
        0, fields.at[:, 0:HALO, :], fields.at[:, rows : rows + HALO, :], (above, lon)
    )
    high_rows = edge_copy(
        1,
        fields.at[:, rows - HALO : rows, :],
        fields.at[:, rows + HALO : rows + 2 * HALO, :],
        (below, lon),
    )
    low_leg = edge_copy(
        2, legendre_ref.at[:, 0:HALO, :], leg_halo.at[:, 0:HALO, :], (above, lon)
    )
    high_leg = edge_copy(
        3,
        legendre_ref.at[:, rows - HALO : rows, :],
        leg_halo.at[:, HALO : 2 * HALO, :],
        (below, lon),
    )

    @pl.when(lat > 0)
    def _():
        low_rows.start()
        low_leg.start()

    @pl.when(lat < n_lat - 1)
    def _():
        high_rows.start()
        high_leg.start()

    @pl.when(lat == 0)
    def _():
        fields[:, rows + HALO : rows + 2 * HALO, :] = jnp.zeros((4, HALO, width), jnp.float32)
        leg_halo[:, HALO : 2 * HALO, :] = jnp.zeros((own, HALO, leg_halo.shape[2]), jnp.float32)

    @pl.when(lat == n_lat - 1)
    def _():
        fields[:, rows : rows + HALO, :] = jnp.zeros((4, HALO, width), jnp.float32)
        leg_halo[:, 0:HALO, :] = jnp.zeros((own, HALO, leg_halo.shape[2]), jnp.float32)

    leg_copy.wait()
    all_received(0, a_in, n_lon - 1)
    fourier = jnp.sum(a_in[...], axis=0)

    degrees = leg_own.shape[2]
    lane8 = lax.broadcasted_iota(jnp.int32, (8, LANES), 1)
    row8 = lax.broadcasted_iota(jnp.int32, (8, LANES), 0)
    both = jnp.concatenate([fourier, fourier], axis=0)
    swapped = pltpu.roll(both, rows, 1)
    spread = jnp.where((lane8 < rows) == (row8 < 4), both, swapped)
    wave8 = jnp.bitwise_and(row8, 3)
    left = jnp.concatenate(
        [jnp.where(wave8 == 2 * h + lane8 // rows, spread, 0.0) for h in range(own * rows // LANES)],
        axis=1,
    )
    part = dot(left, leg_own[...].reshape(own * rows, degrees), ((1,), (0,)))
    for i in range(n_lat):
        b_out[i] = part[:, LANES * i : LANES * (i + 1)]
    for other in lats:
        lat_copy(1, b_out.at[other], b_in.at[lat], other).start()
    b_in[lat] = b_out[lat]

    @pl.when(lat > 0)
    def _():
        high_rows.wait_recv()

    @pl.when(lat < n_lat - 1)
    def _():
        low_rows.wait_recv()

    deep = fields.shape[1]
    lane80 = lax.broadcasted_iota(jnp.int32, (deep, LANES), 1)
    packed_left = jnp.zeros((deep, LANES), jnp.float32)
    packed_right = jnp.zeros((deep, LANES), jnp.float32)
    for f in range(4):
        here = (lane80 >= 16 * f) & (lane80 < 16 * f + HALO)
        west = fields[f, :, 0:LANES]
        east = fields[f, :, base : base + LANES]
        packed_left = jnp.where(here, pltpu.roll(west, 16 * f, 1), packed_left)
        packed_right = jnp.where(
            here, pltpu.roll(east, (16 * f - (rest - HALO)) % LANES, 1), packed_right
        )
    to_left[...] = packed_left
    to_right[...] = packed_right
    west_side, east_side = lax.rem(lon + n_lon - 1, n_lon), lax.rem(lon + 1, n_lon)
    left_copy = edge_copy(4, to_left, from_right, (lat, west_side))
    right_copy = edge_copy(5, to_right, from_left, (lat, east_side))
    left_copy.start()
    right_copy.start()

    all_received(1, b_in, n_lat - 1)

    c_out[...] = jnp.sum(b_in[...], axis=0)
    for other in lats:
        lat_copy(2, c_out, c_in.at[lat], other).start()
    c_in[lat] = c_out[...]

    @pl.when(lat > 0)
    def _():
        low_rows.wait_send()

    @pl.when(lat < n_lat - 1)
    def _():
        high_rows.wait_send()

    left_copy.wait_recv()
    right_copy.wait_recv()
    right_halo = from_right[...]
    left_halo = from_left[...]
    for f in range(4):
        tile = fields[f, :, base : base + LANES]
        tile = jnp.where(
            (lane80 >= rest) & (lane80 < rest + HALO),
            pltpu.roll(right_halo, (rest - 16 * f) % LANES, 1),
            tile,
        )
        tile = jnp.where(
            lane80 >= LANES - HALO,
            pltpu.roll(left_halo, (LANES - HALO - 16 * f) % LANES, 1),
            tile,
        )
        fields[f, :, base : base + LANES] = tile

    @pl.when(lat > 0)
    def _():
        high_leg.wait_recv()

    @pl.when(lat < n_lat - 1)
    def _():
        low_leg.wait_recv()

    all_received(2, c_in, n_lat - 1)

    spectral = jnp.concatenate([c_in[i] for i in range(n_lat)], axis=1) * love_ref[...]
    inner = dot(spectral, leg_own[...].reshape(own * rows, degrees), ((1,), (1,)))
    outer = dot(spectral, leg_halo[...].reshape(own * 2 * HALO, degrees), ((1,), (1,)))
    body = jnp.zeros((8, LANES), jnp.float32)
    for h in range(own * rows // LANES):
        body = body + jnp.where(
            wave8 == 2 * h + lane8 // rows, inner[:, LANES * h : LANES * (h + 1)], 0.0
        )
    body = body + pltpu.roll(body, rows, 1)
    rim = jnp.concatenate(
        [outer, jnp.zeros((8, LANES - own * 2 * HALO), jnp.float32)], axis=1
    )
    rim = jnp.where(wave8 == lane8 // (2 * HALO), rim, 0.0)
    folded = pltpu.roll(rim, rows, 1)
    for m in range(1, own):
        folded = folded + pltpu.roll(rim, rows - 2 * HALO * m, 1)
    synthesized = jnp.where(
        lane8 < rows, body, jnp.where(lane8 < rows + 2 * HALO, folded, 0.0)
    )
    d_out[...] = synthesized * (1.0 / math.sqrt(count))
    for other in lons:
        lon_copy(3, d_out, d_in.at[lon], other).start()
    d_in[lon] = d_out[...]
    all_received(3, d_in, n_lon - 1)

    loading = dot(d_in[...].reshape(8 * n_lon, LANES), harmonics[...], ((0,), (0,)))[0:deep]

    surface = fields[0]
    east = fields[1]
    north = fields[2]
    wet = fields[3]
    wide, tall = width - 1, deep - 1
    for _ in range(SUBSTEPS):
        pressure = surface - loading
        east = wet * (
            east - EAST_STEP * (pltpu.roll(pressure, wide, 1) - pltpu.roll(pressure, 1, 1))
        )
        north = wet * (
            north - NORTH_STEP * (pltpu.roll(pressure, tall, 0) - pltpu.roll(pressure, 1, 0))
        )
        change = EAST_STEP * (pltpu.roll(east, wide, 1) - pltpu.roll(east, 1, 1)) + NORTH_STEP * (
            pltpu.roll(north, tall, 0) - pltpu.roll(north, 1, 0)
        )
        surface = surface - wet * change
    loading_out[...] = loading[0:rows, 0:cols]
    surface_out[...] = surface[0:rows, 0:cols]
    east_out_ref[...] = east[0:rows, 0:cols]
    north_out_ref[...] = north[0:rows, 0:cols]

    all_sent(0, a_in, n_lon - 1)
    all_sent(1, b_in, n_lat - 1)
    all_sent(2, c_in, n_lat - 1)
    all_sent(3, d_in, n_lon - 1)
    left_copy.wait_send()
    right_copy.wait_send()

    @pl.when(lat > 0)
    def _():
        low_leg.wait_send()

    @pl.when(lat < n_lat - 1)
    def _():
        high_leg.wait_send()


def shards(height, east_flow, north_flow, legendre, love_numbers, wavenumbers, land_sea):
    n_lat, n_lon = lax.axis_size("lat"), lax.axis_size("lon")
    rows, cols = height.shape
    own, _, degrees = legendre.shape
    width = -(-(cols + 2 * HALO) // LANES) * LANES
    deep = rows + 2 * HALO
    vmem = pl.BlockSpec(memory_space=pltpu.VMEM)
    f32 = jnp.float32
    shape = jax.ShapeDtypeStruct((rows, cols), f32)
    return pl.pallas_call(
        functools.partial(kernel, n_lat, n_lon),
        out_shape=(shape, shape, shape, shape),
        in_specs=[vmem, vmem, vmem, vmem, pl.BlockSpec(memory_space=pl.ANY), vmem, vmem],
        out_specs=(vmem, vmem, vmem, vmem),
        scratch_shapes=[
            pltpu.VMEM((4, deep, width), f32),
            pltpu.VMEM((8 * n_lon, width), f32),
            pltpu.VMEM((2 * rows, width), f32),
            pltpu.VMEM((own, rows, degrees), f32),
            pltpu.VMEM((own, 2 * HALO, degrees), f32),
            pltpu.VMEM((n_lon, own, LANES), f32),
            pltpu.VMEM((n_lon, own, LANES), f32),
            pltpu.VMEM((n_lat, 8, LANES), f32),
            pltpu.VMEM((n_lat, 8, LANES), f32),
            pltpu.VMEM((8, LANES), f32),
            pltpu.VMEM((n_lat, 8, LANES), f32),
            pltpu.VMEM((8, LANES), f32),
            pltpu.VMEM((n_lon, 8, LANES), f32),
            pltpu.VMEM((deep, LANES), f32),
            pltpu.VMEM((deep, LANES), f32),
            pltpu.VMEM((deep, LANES), f32),
            pltpu.VMEM((deep, LANES), f32),
            pltpu.SemaphoreType.DMA,
            pltpu.SemaphoreType.DMA((4,)),
            pltpu.SemaphoreType.DMA((4,)),
            pltpu.SemaphoreType.DMA((6,)),
            pltpu.SemaphoreType.DMA((6,)),
        ],
        compiler_params=pltpu.CompilerParams(collective_id=0, has_side_effects=True),
    )(
        height,
        east_flow,
        north_flow,
        land_sea,
        legendre,
        love_numbers.reshape(1, degrees),
        wavenumbers.reshape(1, wavenumbers.shape[0]),
    )


def solution(mesh):
    return jax.shard_map(
        shards,
        mesh=mesh,
        in_specs=(
            P("lat", "lon"),
            P("lat", "lon"),
            P("lat", "lon"),
            P("lon", "lat", None),
            P(),
            P(),
            P("lat", "lon"),
        ),
        out_specs=(P("lat", "lon"), P("lat", "lon"), P("lat", "lon"), P("lat", "lon")),
        check_vma=False,
    )
```

time: 584 us -> 53 us (0.09)
  the two profiles are of different devices: /device:TPU:56 before, /device:TPU:1 now
where the time goes in v1:
time: 53 us; the launch traced here: 52.7 us
  Pallas kernels  45.9 us (87%)
  local copies, waits for them, and re-layouts  6.16 us (12%)
  between operations  0.64 us (1%)
    pallas_call x1, Pallas kernels, shards(): pl.pallas_call(functools.partial(kernel, n_lat, n_lon), out_shape=(shape,...  45.9 us
    unnamed x4, local copies, waits for them, and re-layouts  6.16 us

profile of v1, /device:TPU:1, one launch (start us, length us, event | category | flops | bytes accessed | tf_op | source)
XLA Modules:
  0.0 52.7 jit_solution(3880975252746215522)
XLA Ops:
  0.6 45.9 %shard_map.102 = (f32[64,270]{1,0:T(8,128)}, f32[64,270]{1,0:T(8,128)}, f32[64,270]{1,0:T(8,128)}, f32[64,270]{1,0:T(8,128)}) custom-call(f32[64,270]{1,0:T(8,128)} %height_ref.1, f32[64,270]{1,0:T(8,128)} %east_ref.1, f32[64,270]{1,0:T(8,128)} %north_ref.1, s32[64,270]{1,0:T(8,128)} %land_ref.1, f32[4,64,2048]{2,1,0:T(8,128)} %legendre_ref.1, ...), custom_call_target="tpu_custom_call" | custom-call | tf_op jit(solution)/shard_map/pallas_call | solution.py:399
  46.5 1.5 %copy.15 = f32[64,270]{1,0:T(8,128)} copy(f32[64,270]{1,0:T(8,128)} %get-tuple-element.8) | data formatting | bytes 138240
  48.1 1.5 %copy.16 = f32[64,270]{1,0:T(8,128)} copy(f32[64,270]{1,0:T(8,128)} %get-tuple-element.9) | data formatting | bytes 138240
  49.6 1.5 %copy.17 = f32[64,270]{1,0:T(8,128)} copy(f32[64,270]{1,0:T(8,128)} %get-tuple-element.10) | data formatting | bytes 138240
  51.2 1.5 %copy.18 = f32[64,270]{1,0:T(8,128)} copy(f32[64,270]{1,0:T(8,128)} %get-tuple-element.11) | data formatting | bytes 138240

commit v2 on v1

--- a/solution.py
+++ b/solution.py
@@ -46,17 +46,23 @@
 def kernel(
     n_lat,
     n_lon,
+    height_hbm,
+    east_hbm,
+    north_hbm,
+    land_hbm,
+    legendre_ref,
+    love_hbm,
+    waves_hbm,
+    loading_out,
+    surface_out,
+    east_out_ref,
+    north_out_ref,
     height_ref,
     east_ref,
     north_ref,
     land_ref,
-    legendre_ref,
     love_ref,
     waves_ref,
-    loading_out,
-    surface_out,
-    east_out_ref,
-    north_out_ref,
     fields,
     harmonics,
     twice,
@@ -74,7 +80,7 @@
     to_right,
     from_right,
     from_left,
-    leg_sem,
+    in_sem,
     send_sem,
     recv_sem,
     edge_send,
@@ -90,13 +96,29 @@
     lats = lat_partners(n_lat, lat)
     lons = lon_partners(n_lon, lon)
 
+    inputs = [
+        pltpu.make_async_copy(src, dst, in_sem.at[k])
+        for k, (src, dst) in enumerate(
+            (
+                (waves_hbm, waves_ref),
+                (height_hbm, height_ref),
+                (east_hbm, east_ref),
+                (north_hbm, north_ref),
+                (land_hbm, land_ref),
+                (love_hbm, love_ref),
+                (legendre_ref, leg_own),
+            )
+        )
+    ]
+    for copy in inputs:
+        copy.start()
     barrier = pltpu.get_barrier_semaphore()
     for other in lons:
         pl.semaphore_signal(barrier, inc=1, device_id=(lat, other), device_id_type=MESH)
     for other in lats:
         pl.semaphore_signal(barrier, inc=1, device_id=(other, lon), device_id_type=MESH)
-    leg_copy = pltpu.make_async_copy(legendre_ref, leg_own, leg_sem)
-    leg_copy.start()
+    for copy in inputs[:6]:
+        copy.wait()
 
     for f, ref in enumerate((height_ref, east_ref, north_ref, land_ref)):
         fields[f, 0:rows, base:width] = jnp.zeros((rows, width - base), jnp.float32)
@@ -229,7 +251,7 @@
         fields[:, rows : rows + HALO, :] = jnp.zeros((4, HALO, width), jnp.float32)
         leg_halo[:, 0:HALO, :] = jnp.zeros((own, HALO, leg_halo.shape[2]), jnp.float32)
 
-    leg_copy.wait()
+    inputs[6].wait()
     all_received(0, a_in, n_lon - 1)
     fourier = jnp.sum(a_in[...], axis=0)
 
@@ -387,6 +409,15 @@
         high_leg.wait_send()
 
 
+def write_kernel(a_ref, b_ref, c_ref, d_ref, a_out, b_out, c_out, d_out, sem):
+    pairs = ((a_ref, a_out), (b_ref, b_out), (c_ref, c_out), (d_ref, d_out))
+    copies = [pltpu.make_async_copy(src, dst, sem.at[k]) for k, (src, dst) in enumerate(pairs)]
+    for copy in copies:
+        copy.start()
+    for copy in copies:
+        copy.wait()
+
+
 def shards(height, east_flow, north_flow, legendre, love_numbers, wavenumbers, land_sea):
     n_lat, n_lon = lax.axis_size("lat"), lax.axis_size("lon")
     rows, cols = height.shape
@@ -396,12 +427,19 @@
     vmem = pl.BlockSpec(memory_space=pltpu.VMEM)
     f32 = jnp.float32
     shape = jax.ShapeDtypeStruct((rows, cols), f32)
-    return pl.pallas_call(
+    held = pltpu.VMEM((rows, cols), f32)
+    results = pl.pallas_call(
         functools.partial(kernel, n_lat, n_lon),
-        out_shape=(shape, shape, shape, shape),
-        in_specs=[vmem, vmem, vmem, vmem, pl.BlockSpec(memory_space=pl.ANY), vmem, vmem],
+        out_shape=(held, held, held, held),
+        in_specs=[pl.BlockSpec(memory_space=pltpu.HBM)] * 7,
         out_specs=(vmem, vmem, vmem, vmem),
         scratch_shapes=[
+            held,
+            held,
+            held,
+            pltpu.VMEM((rows, cols), jnp.int32),
+            pltpu.VMEM((1, degrees), f32),
+            pltpu.VMEM((1, wavenumbers.shape[0]), jnp.int32),
             pltpu.VMEM((4, deep, width), f32),
             pltpu.VMEM((8 * n_lon, width), f32),
             pltpu.VMEM((2 * rows, width), f32),
@@ -419,22 +457,38 @@
             pltpu.VMEM((deep, LANES), f32),
             pltpu.VMEM((deep, LANES), f32),
             pltpu.VMEM((deep, LANES), f32),
-            pltpu.SemaphoreType.DMA,
+            pltpu.SemaphoreType.DMA((7,)),
             pltpu.SemaphoreType.DMA((4,)),
             pltpu.SemaphoreType.DMA((4,)),
             pltpu.SemaphoreType.DMA((6,)),
             pltpu.SemaphoreType.DMA((6,)),
         ],
-        compiler_params=pltpu.CompilerParams(collective_id=0, has_side_effects=True),
+        compiler_params=pltpu.CompilerParams(
+            collective_id=0, has_side_effects=True, vmem_limit_bytes=24 << 20
+        ),
     )(
-        height,
-        east_flow,
-        north_flow,
-        land_sea,
-        legendre,
-        love_numbers.reshape(1, degrees),
-        wavenumbers.reshape(1, wavenumbers.shape[0]),
-    )
+        *[
+            pltpu.with_memory_space_constraint(x, pltpu.HBM)
+            for x in (
+                height,
+                east_flow,
+                north_flow,
+                land_sea,
+                legendre,
+                love_numbers.reshape(1, degrees),
+                wavenumbers.reshape(1, wavenumbers.shape[0]),
+            )
+        ]
+    )
+    anywhere = pl.BlockSpec(memory_space=pl.ANY)
+    return pl.pallas_call(
+        write_kernel,
+        out_shape=(shape, shape, shape, shape),
+        in_specs=[vmem, vmem, vmem, vmem],
+        out_specs=(anywhere, anywhere, anywhere, anywhere),
+        scratch_shapes=[pltpu.SemaphoreType.DMA((4,))],
+        compiler_params=pltpu.CompilerParams(vmem_limit_bytes=8 << 20),
+    )(*results)
 
 
 def solution(mesh):

time: 53 us -> 46 us (0.87)
  local copies, waits for them, and re-layouts: 6.16 us -> 0 us
  Pallas kernels: 45.9 us -> 45.2 us
    unnamed x4 -> x0, local copies, waits for them, and re-layouts: 6.16 us -> none
    pallas_call x1 -> x2, Pallas kernels: 45.9 us -> 45.2 us  [the longest x1 44.4 us: shards(): pl.pallas_call(functools.partial(kernel, n_lat, n_lon), out_shape=(held,...]
where the time goes in v2:
time: 46 us; the launch traced here: 45.8 us
  Pallas kernels  45.2 us (98%)
  between operations  0.64 us (1%)
    pallas_call x1, Pallas kernels, shards(): pl.pallas_call(functools.partial(kernel, n_lat, n_lon), out_shape=(held,...  44.4 us

profile of v2, /device:TPU:1, one launch (start us, length us, event | category | flops | bytes accessed | tf_op | source)
XLA Modules:
  0.0 45.8 jit_solution(6759644090823150493)
XLA Ops:
  0.6 44.4 %shard_map.102 = (f32[64,270]{1,0:T(8,128)S(1)}, f32[64,270]{1,0:T(8,128)S(1)}, f32[64,270]{1,0:T(8,128)S(1)}, f32[64,270]{1,0:T(8,128)S(1)}) custom-call(f32[64,270]{1,0:T(8,128)} %height_hbm.1, f32[64,270]{1,0:T(8,128)} %east_hbm.1, f32[64,270]{1,0:T(8,128)} %north_hbm.1, s32[64,270]{1,0:T(8,128)} %land_hbm.1, f32[4,64,2048]{2,1,0:T(8,128)} %legendre_ref.1, ...), custom_call_target="tpu_custom_call" | custom-call | tf_op jit(solution)/shard_map/pallas_call | solution.py:431
  45.1 0.8 %shard_map.103 = (f32[64,270]{1,0:T(8,128)}, f32[64,270]{1,0:T(8,128)}, f32[64,270]{1,0:T(8,128)}, f32[64,270]{1,0:T(8,128)}) custom-call(f32[64,270]{1,0:T(8,128)S(1)} %get-tuple-element.8.a_ref, f32[64,270]{1,0:T(8,128)S(1)} %get-tuple-element.9.b_ref, f32[64,270]{1,0:T(8,128)S(1)} %get-tuple-element.10.c_ref, f32[64,270]{1,0:T(8,128)S(1)} %get-tuple-element.11.d_ref), custom_call_target="tpu_custom_call" | custom-call | tf_op jit(solution)/shard_map/pallas_call | solution.py:484

commit v3 on v2

--- a/solution.py
+++ b/solution.py
@@ -11,15 +11,22 @@
 SUBSTEPS = 4
 HALO = 2 * SUBSTEPS
 LANES = 128
-EAST_STEP = 0.3
-NORTH_STEP = 0.3
+STEP = 0.3
 MESH = pl.DeviceIdType.MESH
-HIGHEST = lax.Precision.HIGHEST
 
 
 def dot(a, b, dims):
-    return lax.dot_general(
-        a, b, (dims, ((), ())), precision=HIGHEST, preferred_element_type=jnp.float32
+    return lax.dot_general(a, b, (dims, ((), ())), preferred_element_type=jnp.float32)
+
+
+def split(x):
+    high = x.astype(jnp.bfloat16)
+    return high, (x - high.astype(jnp.float32)).astype(jnp.bfloat16)
+
+
+def stacked(x):
+    return jnp.concatenate([x, x - x.astype(jnp.bfloat16).astype(jnp.float32)], axis=0).astype(
+        jnp.bfloat16
     )
 
 
@@ -64,9 +71,12 @@
     love_ref,
     waves_ref,
     fields,
-    harmonics,
-    twice,
+    by_slot,
+    harm_high,
+    harm_low,
     leg_own,
+    leg_high,
+    leg_low,
     leg_halo,
     a_out,
     a_in,
@@ -123,19 +133,21 @@
     for f, ref in enumerate((height_ref, east_ref, north_ref, land_ref)):
         fields[f, 0:rows, base:width] = jnp.zeros((rows, width - base), jnp.float32)
         fields[f, 0:rows, 0:cols] = ref[...].astype(jnp.float32)
-    twice[0:rows, :] = fields[0, 0:rows, :]
-    twice[rows : 2 * rows, :] = fields[0, 0:rows, :]
+    high, low = split(fields[0, 0:rows, :])
+    twice_high = jnp.concatenate([high, high], axis=0)
+    twice_low = jnp.concatenate([low, low], axis=0)
 
     count = waves_ref.shape[1]
-    waves = jnp.broadcast_to(waves_ref[...].astype(jnp.float32), (LANES, count)).T
+    by_slot[...] = jnp.broadcast_to(waves_ref[...].astype(jnp.float32), (LANES, count)).T
+    waves = jnp.concatenate([by_slot[pl.ds(m, n_lon, stride=own), :] for m in range(own)], axis=0)
     start = jnp.bitwise_and(waves.astype(jnp.int32) * lon, n_lon - 1).astype(jnp.float32) * cols
     quarter = period // 4
-    lane = lax.broadcasted_iota(jnp.int32, (8, width), 1)
+    lane = lax.broadcasted_iota(jnp.int32, (16, width), 1)
     column = jnp.where(lane < width - 64, lane, lane - width).astype(jnp.float32)
-    upper = lax.broadcasted_iota(jnp.int32, (8, width), 0) < 4
-    for g in range(count // 8):
-        wave = jnp.concatenate([waves[8 * g : 8 * g + 8]] * (width // LANES), axis=1)
-        first = jnp.concatenate([start[8 * g : 8 * g + 8]] * (width // LANES), axis=1)
+    for g in range(count // 16):
+        here = slice(16 * g, 16 * g + 16)
+        wave = jnp.concatenate([waves[here]] * (width // LANES), axis=1)
+        first = jnp.concatenate([start[here]] * (width // LANES), axis=1)
         r = wave * column + first
         turn = (r * (1.0 / quarter) + 4096.5).astype(jnp.int32)
         d = r - (turn - 4096).astype(jnp.float32) * quarter
@@ -159,14 +171,19 @@
         c = jnp.where(cos_minus, -c, c)
         n = jnp.where(odd, cos, sin)
         n = jnp.where(sin_minus, -n, n)
-        harmonics[16 * g : 16 * g + 8, :] = jnp.where(upper, c, pltpu.roll(n, 4, 0))
-        harmonics[16 * g + 8 : 16 * g + 16, :] = jnp.where(upper, pltpu.roll(c, 4, 0), n)
-
-    partial = dot(harmonics[...], twice[...], ((1,), (1,))) * (1.0 / math.sqrt(period))
-    half = lax.broadcasted_iota(jnp.int32, (8, LANES), 1) < rows
-    for j in range(n_lon):
-        block = partial[8 * j : 8 * j + 8]
-        a_out[j] = jnp.where(half, block, pltpu.roll(block, 4, 0))[0:4]
+        there = slice(count + 16 * g, count + 16 * g + 16)
+        harm_high[here, :], harm_low[here, :] = split(c)
+        harm_high[there, :], harm_low[there, :] = split(n)
+
+    partial = (
+        dot(harm_high[...], twice_high, ((1,), (1,)))
+        + dot(harm_high[...], twice_low, ((1,), (1,)))
+        + dot(harm_low[...], twice_high, ((1,), (1,)))
+    )
+    half = lax.broadcasted_iota(jnp.int32, (count, LANES), 1) < rows
+    partial = jnp.where(half, partial[0:count], partial[count : 2 * count])
+    for m in range(own):
+        a_out[:, m, :] = partial[n_lon * m : n_lon * (m + 1)]
 
     pl.semaphore_wait(barrier, n_lat + n_lon - 2)
 
@@ -252,8 +269,12 @@
         leg_halo[:, 0:HALO, :] = jnp.zeros((own, HALO, leg_halo.shape[2]), jnp.float32)
 
     inputs[6].wait()
+    inner_rows = own * rows
+    for m in range(own):
+        here = slice(rows * m, rows * (m + 1))
+        leg_high[here, :], leg_low[here, :] = split(leg_own[m])
     all_received(0, a_in, n_lon - 1)
-    fourier = jnp.sum(a_in[...], axis=0)
+    fourier = jnp.sum(a_in[...], axis=0) * (1.0 / math.sqrt(period))
 
     degrees = leg_own.shape[2]
     lane8 = lax.broadcasted_iota(jnp.int32, (8, LANES), 1)
@@ -266,7 +287,9 @@
         [jnp.where(wave8 == 2 * h + lane8 // rows, spread, 0.0) for h in range(own * rows // LANES)],
         axis=1,
     )
-    part = dot(left, leg_own[...].reshape(own * rows, degrees), ((1,), (0,)))
+    left = stacked(left)
+    part = dot(left, leg_high[0:inner_rows, :], ((1,), (0,)))
+    part = part[0:8] + part[8:16] + dot(left[0:8], leg_low[0:inner_rows, :], ((1,), (0,)))
     for i in range(n_lat):
         b_out[i] = part[:, LANES * i : LANES * (i + 1)]
     for other in lats:
@@ -342,52 +365,80 @@
     def _():
         low_leg.wait_recv()
 
+    both_leg = split(leg_halo[...].reshape(own * 2 * HALO, degrees))
+    leg_high[inner_rows:, :], leg_low[inner_rows:, :] = both_leg
     all_received(2, c_in, n_lat - 1)
 
     spectral = jnp.concatenate([c_in[i] for i in range(n_lat)], axis=1) * love_ref[...]
-    inner = dot(spectral, leg_own[...].reshape(own * rows, degrees), ((1,), (1,)))
-    outer = dot(spectral, leg_halo[...].reshape(own * 2 * HALO, degrees), ((1,), (1,)))
+    spectral = stacked(spectral)
+    values = dot(spectral, leg_high[...], ((1,), (1,)))
+    values = values[0:8] + values[8:16] + dot(spectral[0:8], leg_low[...], ((1,), (1,)))
     body = jnp.zeros((8, LANES), jnp.float32)
-    for h in range(own * rows // LANES):
+    for h in range(inner_rows // LANES):
         body = body + jnp.where(
-            wave8 == 2 * h + lane8 // rows, inner[:, LANES * h : LANES * (h + 1)], 0.0
+            wave8 == 2 * h + lane8 // rows, values[:, LANES * h : LANES * (h + 1)], 0.0
         )
     body = body + pltpu.roll(body, rows, 1)
+    body = jnp.where(lane8 < rows, body, pltpu.roll(body, 4, 0))
     rim = jnp.concatenate(
-        [outer, jnp.zeros((8, LANES - own * 2 * HALO), jnp.float32)], axis=1
+        [values[:, inner_rows:], jnp.zeros((8, LANES - own * 2 * HALO), jnp.float32)], axis=1
     )
     rim = jnp.where(wave8 == lane8 // (2 * HALO), rim, 0.0)
-    folded = pltpu.roll(rim, rows, 1)
-    for m in range(1, own):
-        folded = folded + pltpu.roll(rim, rows - 2 * HALO * m, 1)
-    synthesized = jnp.where(
-        lane8 < rows, body, jnp.where(lane8 < rows + 2 * HALO, folded, 0.0)
-    )
-    d_out[...] = synthesized * (1.0 / math.sqrt(count))
+    rim = jnp.where(row8 < 4, rim, pltpu.roll(rim, own * 2 * HALO, 1))
+    rim = jnp.sum(rim, axis=0, keepdims=True)
+    packet = jnp.where(row8 < 4, body, rim) * (1.0 / math.sqrt(count))
+    d_out[...] = packet[0:5]
     for other in lons:
         lon_copy(3, d_out, d_in.at[lon], other).start()
     d_in[lon] = d_out[...]
+
+    wet = fields[3]
+    fields[1] = fields[1] * wet
+    fields[2] = fields[2] * wet
+    fields[3] = wet * STEP
     all_received(3, d_in, n_lon - 1)
 
-    loading = dot(d_in[...].reshape(8 * n_lon, LANES), harmonics[...], ((0,), (0,)))[0:deep]
-
-    surface = fields[0]
+    rows_kt = jnp.concatenate([d_in[:, m, :] for m in range(own)], axis=0)
+    rows_tk = rows_kt.T
+    rim_kt = jnp.concatenate(
+        [d_in[:, 4, :], jnp.zeros((count - n_lon, LANES), jnp.float32)], axis=0
+    )
+    rim_tk = rim_kt.T
+    rims = []
+    for p in range(2):
+        side = rim_tk[2 * HALO * own * p : 2 * HALO * (own * p + 1)]
+        for m in range(1, own):
+            first = 2 * HALO * (own * p + m)
+            side = side + pltpu.roll(rim_tk[first : first + 2 * HALO], n_lon * m, 1)
+        rims.append(side)
+    coefficients = jnp.concatenate(
+        [
+            jnp.concatenate([rows_tk[0:rows], rows_tk[rows : 2 * rows]], axis=1),
+            jnp.concatenate(rims, axis=1),
+        ],
+        axis=0,
+    )
+    coefficients = stacked(coefficients)
+    loading = dot(coefficients, harm_high[...], ((1,), (0,)))
+    loading = (
+        loading[0:deep]
+        + loading[deep : 2 * deep]
+        + dot(coefficients[0:deep], harm_low[...], ((1,), (0,)))
+    )
+
+    pressure = fields[0] - loading
     east = fields[1]
     north = fields[2]
-    wet = fields[3]
+    step = fields[3]
     wide, tall = width - 1, deep - 1
     for _ in range(SUBSTEPS):
-        pressure = surface - loading
-        east = wet * (
-            east - EAST_STEP * (pltpu.roll(pressure, wide, 1) - pltpu.roll(pressure, 1, 1))
-        )
-        north = wet * (
-            north - NORTH_STEP * (pltpu.roll(pressure, tall, 0) - pltpu.roll(pressure, 1, 0))
-        )
-        change = EAST_STEP * (pltpu.roll(east, wide, 1) - pltpu.roll(east, 1, 1)) + NORTH_STEP * (
-            pltpu.roll(north, tall, 0) - pltpu.roll(north, 1, 0)
-        )
-        surface = surface - wet * change
+        east = east - step * (pltpu.roll(pressure, wide, 1) - pltpu.roll(pressure, 1, 1))
+        north = north - step * (pltpu.roll(pressure, tall, 0) - pltpu.roll(pressure, 1, 0))
+        pressure = pressure - step * (
+            (pltpu.roll(east, wide, 1) - pltpu.roll(east, 1, 1))
+            + (pltpu.roll(north, tall, 0) - pltpu.roll(north, 1, 0))
+        )
+    surface = pressure + loading
     loading_out[...] = loading[0:rows, 0:cols]
     surface_out[...] = surface[0:rows, 0:cols]
     east_out_ref[...] = east[0:rows, 0:cols]
@@ -441,9 +492,12 @@
             pltpu.VMEM((1, degrees), f32),
             pltpu.VMEM((1, wavenumbers.shape[0]), jnp.int32),
             pltpu.VMEM((4, deep, width), f32),
-            pltpu.VMEM((8 * n_lon, width), f32),
-            pltpu.VMEM((2 * rows, width), f32),
+            pltpu.VMEM((own * n_lon, LANES), f32),
+            pltpu.VMEM((2 * own * n_lon, width), jnp.bfloat16),
+            pltpu.VMEM((2 * own * n_lon, width), jnp.bfloat16),
             pltpu.VMEM((own, rows, degrees), f32),
+            pltpu.VMEM((own * deep, degrees), jnp.bfloat16),
+            pltpu.VMEM((own * deep, degrees), jnp.bfloat16),
             pltpu.VMEM((own, 2 * HALO, degrees), f32),
             pltpu.VMEM((n_lon, own, LANES), f32),
             pltpu.VMEM((n_lon, own, LANES), f32),
@@ -451,8 +505,8 @@
             pltpu.VMEM((n_lat, 8, LANES), f32),
             pltpu.VMEM((8, LANES), f32),
             pltpu.VMEM((n_lat, 8, LANES), f32),
-            pltpu.VMEM((8, LANES), f32),
-            pltpu.VMEM((n_lon, 8, LANES), f32),
+            pltpu.VMEM((5, LANES), f32),
+            pltpu.VMEM((n_lon, 5, LANES), f32),
             pltpu.VMEM((deep, LANES), f32),
             pltpu.VMEM((deep, LANES), f32),
             pltpu.VMEM((deep, LANES), f32),

time: 46 us -> 43.5 us (0.946)
  Pallas kernels: 45.2 us -> 42.7 us
    pallas_call x1, Pallas kernels: 44.4 us -> 42 us  [shards(): pl.pallas_call(functools.partial(kernel, n_lat, n_lon), out_shape=(held,...]
where the time goes in v3:
time: 43.5 us; the launch traced here: 43.4 us
  Pallas kernels  42.7 us (98%)
  between operations  0.64 us (1%)
    pallas_call x1, Pallas kernels, shards(): pl.pallas_call(functools.partial(kernel, n_lat, n_lon), out_shape=(held,...  42 us

profile of v3, /device:TPU:1, one launch (start us, length us, event | category | flops | bytes accessed | tf_op | source)
XLA Modules:
  0.0 43.4 jit_solution(16967429661486212058)
XLA Ops:
  0.6 42.0 %shard_map.102 = (f32[64,270]{1,0:T(8,128)S(1)}, f32[64,270]{1,0:T(8,128)S(1)}, f32[64,270]{1,0:T(8,128)S(1)}, f32[64,270]{1,0:T(8,128)S(1)}) custom-call(f32[64,270]{1,0:T(8,128)} %height_hbm.1, f32[64,270]{1,0:T(8,128)} %east_hbm.1, f32[64,270]{1,0:T(8,128)} %north_hbm.1, s32[64,270]{1,0:T(8,128)} %land_hbm.1, f32[4,64,2048]{2,1,0:T(8,128)} %legendre_ref.1, ...), custom_call_target="tpu_custom_call" | custom-call | tf_op jit(solution)/shard_map/pallas_call | solution.py:482
  42.6 0.8 %shard_map.103 = (f32[64,270]{1,0:T(8,128)}, f32[64,270]{1,0:T(8,128)}, f32[64,270]{1,0:T(8,128)}, f32[64,270]{1,0:T(8,128)}) custom-call(f32[64,270]{1,0:T(8,128)S(1)} %get-tuple-element.8.a_ref, f32[64,270]{1,0:T(8,128)S(1)} %get-tuple-element.9.b_ref, f32[64,270]{1,0:T(8,128)S(1)} %get-tuple-element.10.c_ref, f32[64,270]{1,0:T(8,128)S(1)} %get-tuple-element.11.d_ref), custom_call_target="tpu_custom_call" | custom-call | tf_op jit(solution)/shard_map/pallas_call | solution.py:538

commit v4 on v3

--- a/solution.py
+++ b/solution.py
@@ -30,24 +30,37 @@
     )
 
 
-def ring_order(n):
-    return sorted(range(n), key=lambda d: -min(d, n - d))
+def hops(n, d):
+    return min(d, n - d)
 
 
 def lat_partners(n_lat, lat):
-    n_y = min(8, n_lat)
-    x_hi, y = lat // n_y, lat % n_y
-    steps = [(dx, dy) for dx in range(n_lat // n_y) for dy in range(n_y) if dx or dy]
-    steps.sort(key=lambda s: -(2 * s[0] + min(s[1], n_y - s[1])))
-    n_x = n_lat // n_y
-    return [((x_hi + dx) % n_x) * n_y + (y + dy) % n_y for dx, dy in steps]
+    n_y = n_lat // 2
+    x_hi, y = lax.div(lat, n_y), lax.rem(lat, n_y)
+    steps = [(2 * dx + hops(n_y, dy), dx, dy) for dx in range(2) for dy in range(n_y)]
+    steps = sorted((step for step in steps if step[0]), reverse=True)
+    return [
+        (far, (1 - x_hi if dx else x_hi) * n_y + lax.rem(y + dy, n_y)) for far, dx, dy in steps
+    ]
 
 
 def lon_partners(n_lon, lon):
     n_z = n_lon // 4
-    z, low = lon // 4, lon % 4
-    steps = [(dz, e) for dz in ring_order(n_z) for e in (2, 3, 1, 0) if dz or e]
-    return [((z + dz) % n_z) * 4 + (low + e) % 4 for dz, e in steps]
+    z, x_lo, core = lax.div(lon, 4), lax.rem(lax.div(lon, 2), 2), lax.rem(lon, 2)
+    steps = [
+        (hops(n_z, dz) + dx, dz, dx, dc)
+        for dz in range(n_z)
+        for dx in range(2)
+        for dc in range(2)
+        if dz or dx or dc
+    ]
+    return [
+        (
+            far,
+            lax.rem(z + dz, n_z) * 4 + (1 - x_lo if dx else x_lo) * 2 + (1 - core if dc else core),
+        )
+        for far, dz, dx, dc in sorted(steps, reverse=True)
+    ]
 
 
 def kernel(
@@ -95,6 +108,8 @@
     recv_sem,
     edge_send,
     edge_recv,
+    c_send,
+    c_recv,
 ):
     lat = lax.axis_index("lat")
     lon = lax.axis_index("lon")
@@ -123,10 +138,12 @@
     for copy in inputs:
         copy.start()
     barrier = pltpu.get_barrier_semaphore()
-    for other in lons:
-        pl.semaphore_signal(barrier, inc=1, device_id=(lat, other), device_id_type=MESH)
-    for other in lats:
-        pl.semaphore_signal(barrier, inc=1, device_id=(other, lon), device_id_type=MESH)
+    everyone = [(far, (other, lon)) for far, other in lats]
+    everyone += [(far, (lat, other)) for far, other in lons]
+    for _, where in sorted(everyone, key=lambda other: -other[0]):
+        pl.semaphore_signal(barrier, inc=1, device_id=where, device_id_type=MESH)
+    n_y = n_lat // 2
+    y = lax.rem(lat, n_y)
     for copy in inputs[:6]:
         copy.wait()
 
@@ -213,7 +230,7 @@
     def all_sent(k, ref, n):
         pltpu.make_async_copy(ref.at[pl.ds(0, n)], ref.at[pl.ds(0, n)], send_sem.at[k]).wait()
 
-    for other in lons:
+    for _, other in lons:
         lon_copy(0, a_out.at[other], a_in.at[lon], other).start()
     a_in[lon] = a_out[lon]
 
@@ -290,11 +307,12 @@
     left = stacked(left)
     part = dot(left, leg_high[0:inner_rows, :], ((1,), (0,)))
     part = part[0:8] + part[8:16] + dot(left[0:8], leg_low[0:inner_rows, :], ((1,), (0,)))
-    for i in range(n_lat):
-        b_out[i] = part[:, LANES * i : LANES * (i + 1)]
-    for other in lats:
-        lat_copy(1, b_out.at[other], b_in.at[lat], other).start()
-    b_in[lat] = b_out[lat]
+    chunk = degrees // n_y
+    for i in range(n_y):
+        b_out[i] = part[:, chunk * i : chunk * (i + 1)]
+    for _, other in lats:
+        lat_copy(1, b_out.at[lax.rem(other, n_y)], b_in.at[lat], other).start()
+    b_in[lat] = b_out[y]
 
     @pl.when(lat > 0)
     def _():
@@ -327,9 +345,20 @@
     all_received(1, b_in, n_lat - 1)
 
     c_out[...] = jnp.sum(b_in[...], axis=0)
-    for other in lats:
-        lat_copy(2, c_out, c_in.at[lat], other).start()
-    c_in[lat] = c_out[...]
+    bands = sorted(range(1, n_y), key=lambda dy: -hops(n_y, dy))
+    c_copies = [
+        pltpu.make_async_remote_copy(
+            src_ref=c_out,
+            dst_ref=c_in.at[y],
+            send_sem=c_send.at[dy],
+            recv_sem=c_recv.at[n_y - dy],
+            device_id=(lat - y + lax.rem(y + dy, n_y), lon),
+            device_id_type=MESH,
+        )
+        for dy in bands
+    ]
+    for copy in c_copies:
+        copy.start()
 
     @pl.when(lat > 0)
     def _():
@@ -367,12 +396,18 @@
 
     both_leg = split(leg_halo[...].reshape(own * 2 * HALO, degrees))
     leg_high[inner_rows:, :], leg_low[inner_rows:, :] = both_leg
-    all_received(2, c_in, n_lat - 1)
-
-    spectral = jnp.concatenate([c_in[i] for i in range(n_lat)], axis=1) * love_ref[...]
-    spectral = stacked(spectral)
-    values = dot(spectral, leg_high[...], ((1,), (1,)))
-    values = values[0:8] + values[8:16] + dot(spectral[0:8], leg_low[...], ((1,), (1,)))
+
+    values = jnp.zeros((16, leg_high.shape[0]), jnp.float32)
+    lows = jnp.zeros((8, leg_high.shape[0]), jnp.float32)
+    for dy in [0] + bands[::-1]:
+        there = lax.rem(y + dy, n_y)
+        if dy:
+            pltpu.make_async_copy(c_out, c_in.at[there], c_recv.at[dy]).wait()
+        block = pl.ds(pl.multiple_of(there * chunk, chunk), chunk)
+        spectral = stacked((c_in[there] if dy else c_out[...]) * love_ref[:, block])
+        values = values + dot(spectral, leg_high[:, block], ((1,), (1,)))
+        lows = lows + dot(spectral[0:8], leg_low[:, block], ((1,), (1,)))
+    values = values[0:8] + values[8:16] + lows
     body = jnp.zeros((8, LANES), jnp.float32)
     for h in range(inner_rows // LANES):
         body = body + jnp.where(
@@ -388,7 +423,7 @@
     rim = jnp.sum(rim, axis=0, keepdims=True)
     packet = jnp.where(row8 < 4, body, rim) * (1.0 / math.sqrt(count))
     d_out[...] = packet[0:5]
-    for other in lons:
+    for _, other in lons:
         lon_copy(3, d_out, d_in.at[lon], other).start()
     d_in[lon] = d_out[...]
 
@@ -446,7 +481,8 @@
 
     all_sent(0, a_in, n_lon - 1)
     all_sent(1, b_in, n_lat - 1)
-    all_sent(2, c_in, n_lat - 1)
+    for copy in c_copies:
+        copy.wait_send()
     all_sent(3, d_in, n_lon - 1)
     left_copy.wait_send()
     right_copy.wait_send()
@@ -475,6 +511,7 @@
     own, _, degrees = legendre.shape
     width = -(-(cols + 2 * HALO) // LANES) * LANES
     deep = rows + 2 * HALO
+    chunk = degrees // (n_lat // 2)
     vmem = pl.BlockSpec(memory_space=pltpu.VMEM)
     f32 = jnp.float32
     shape = jax.ShapeDtypeStruct((rows, cols), f32)
@@ -501,10 +538,10 @@
             pltpu.VMEM((own, 2 * HALO, degrees), f32),
             pltpu.VMEM((n_lon, own, LANES), f32),
             pltpu.VMEM((n_lon, own, LANES), f32),
-            pltpu.VMEM((n_lat, 8, LANES), f32),
-            pltpu.VMEM((n_lat, 8, LANES), f32),
-            pltpu.VMEM((8, LANES), f32),
-            pltpu.VMEM((n_lat, 8, LANES), f32),
+            pltpu.VMEM((n_lat // 2, 8, chunk), f32),
+            pltpu.VMEM((n_lat, 8, chunk), f32),
+            pltpu.VMEM((8, chunk), f32),
+            pltpu.VMEM((n_lat // 2, 8, chunk), f32),
             pltpu.VMEM((5, LANES), f32),
             pltpu.VMEM((n_lon, 5, LANES), f32),
             pltpu.VMEM((deep, LANES), f32),
@@ -516,6 +553,8 @@
             pltpu.SemaphoreType.DMA((4,)),
             pltpu.SemaphoreType.DMA((6,)),
             pltpu.SemaphoreType.DMA((6,)),
+            pltpu.SemaphoreType.DMA((n_lat // 2,)),
+            pltpu.SemaphoreType.DMA((n_lat // 2,)),
         ],
         compiler_params=pltpu.CompilerParams(
             collective_id=0, has_side_effects=True, vmem_limit_bytes=24 << 20

time: 43.5 us -> 42.3 us (0.972)
  Pallas kernels: 42.7 us -> 41.5 us
    pallas_call x1, Pallas kernels: 42 us -> 40.8 us  [shards(): pl.pallas_call(functools.partial(kernel, n_lat, n_lon), out_shape=(held,...]
where the time goes in v4:
time: 42.3 us; the launch traced here: 42.2 us
  Pallas kernels  41.5 us (98%)
  between operations  0.64 us (2%)
    pallas_call x1, Pallas kernels, shards(): pl.pallas_call(functools.partial(kernel, n_lat, n_lon), out_shape=(held,...  40.8 us

profile of v4, /device:TPU:1, one launch (start us, length us, event | category | flops | bytes accessed | tf_op | source)
XLA Modules:
  0.0 42.2 jit_solution(2994340332849142726)
XLA Ops:
  0.6 40.8 %shard_map.102 = (f32[64,270]{1,0:T(8,128)S(1)}, f32[64,270]{1,0:T(8,128)S(1)}, f32[64,270]{1,0:T(8,128)S(1)}, f32[64,270]{1,0:T(8,128)S(1)}) custom-call(f32[64,270]{1,0:T(8,128)} %height_hbm.1, f32[64,270]{1,0:T(8,128)} %east_hbm.1, f32[64,270]{1,0:T(8,128)} %north_hbm.1, s32[64,270]{1,0:T(8,128)} %land_hbm.1, f32[4,64,2048]{2,1,0:T(8,128)} %legendre_ref.1, ...), custom_call_target="tpu_custom_call" | custom-call | tf_op jit(solution)/shard_map/pallas_call | solution.py:519
  41.4 0.8 %shard_map.103 = (f32[64,270]{1,0:T(8,128)}, f32[64,270]{1,0:T(8,128)}, f32[64,270]{1,0:T(8,128)}, f32[64,270]{1,0:T(8,128)}) custom-call(f32[64,270]{1,0:T(8,128)S(1)} %get-tuple-element.8.a_ref, f32[64,270]{1,0:T(8,128)S(1)} %get-tuple-element.9.b_ref, f32[64,270]{1,0:T(8,128)S(1)} %get-tuple-element.10.c_ref, f32[64,270]{1,0:T(8,128)S(1)} %get-tuple-element.11.d_ref), custom_call_target="tpu_custom_call" | custom-call | tf_op jit(solution)/shard_map/pallas_call | solution.py:577

commit v5 on v4

--- a/solution.py
+++ b/solution.py
@@ -84,6 +84,7 @@
     love_ref,
     waves_ref,
     fields,
+    steps,
     by_slot,
     harm_high,
     harm_low,
@@ -305,14 +306,19 @@
         axis=1,
     )
     left = stacked(left)
-    part = dot(left, leg_high[0:inner_rows, :], ((1,), (0,)))
-    part = part[0:8] + part[8:16] + dot(left[0:8], leg_low[0:inner_rows, :], ((1,), (0,)))
     chunk = degrees // n_y
-    for i in range(n_y):
-        b_out[i] = part[:, chunk * i : chunk * (i + 1)]
-    for _, other in lats:
-        lat_copy(1, b_out.at[lax.rem(other, n_y)], b_in.at[lat], other).start()
-    b_in[lat] = b_out[y]
+    bands = sorted(range(1, n_y), key=lambda dy: -hops(n_y, dy))
+    for slot, dy in enumerate(bands + [0]):
+        there = lax.rem(y + dy, n_y)
+        block = pl.ds(pl.multiple_of(there * chunk, chunk), chunk)
+        part = dot(left, leg_high[0:inner_rows, block], ((1,), (0,)))
+        part = part[0:8] + part[8:16] + dot(left[0:8], leg_low[0:inner_rows, block], ((1,), (0,)))
+        b_out[slot] = part
+        lat_copy(1, b_out.at[slot], b_in.at[lat], n_lat - n_y - (lat - y) + there).start()
+        if dy:
+            lat_copy(1, b_out.at[slot], b_in.at[lat], lat - y + there).start()
+        else:
+            b_in[lat] = part
 
     @pl.when(lat > 0)
     def _():
@@ -345,7 +351,6 @@
     all_received(1, b_in, n_lat - 1)
 
     c_out[...] = jnp.sum(b_in[...], axis=0)
-    bands = sorted(range(1, n_y), key=lambda dy: -hops(n_y, dy))
     c_copies = [
         pltpu.make_async_remote_copy(
             src_ref=c_out,
@@ -427,10 +432,14 @@
         lon_copy(3, d_out, d_in.at[lon], other).start()
     d_in[lon] = d_out[...]
 
+    wide, tall = width - 1, deep - 1
     wet = fields[3]
-    fields[1] = fields[1] * wet
-    fields[2] = fields[2] * wet
-    fields[3] = wet * STEP
+    step = wet * STEP
+    fields[1] = pltpu.roll(fields[1] * wet, wide, 1)
+    fields[2] = pltpu.roll(fields[2] * wet, tall, 0)
+    fields[3] = step
+    steps[0] = pltpu.roll(step, wide, 1)
+    steps[1] = pltpu.roll(step, tall, 0)
     all_received(3, d_in, n_lon - 1)
 
     rows_kt = jnp.concatenate([d_in[:, m, :] for m in range(own)], axis=0)
@@ -465,14 +474,14 @@
     east = fields[1]
     north = fields[2]
     step = fields[3]
-    wide, tall = width - 1, deep - 1
     for _ in range(SUBSTEPS):
-        east = east - step * (pltpu.roll(pressure, wide, 1) - pltpu.roll(pressure, 1, 1))
-        north = north - step * (pltpu.roll(pressure, tall, 0) - pltpu.roll(pressure, 1, 0))
+        east = east - steps[0] * (pltpu.roll(pressure, wide - 1, 1) - pressure)
+        north = north - steps[1] * (pltpu.roll(pressure, tall - 1, 0) - pressure)
         pressure = pressure - step * (
-            (pltpu.roll(east, wide, 1) - pltpu.roll(east, 1, 1))
-            + (pltpu.roll(north, tall, 0) - pltpu.roll(north, 1, 0))
-        )
+            (east - pltpu.roll(east, 2, 1)) + (north - pltpu.roll(north, 2, 0))
+        )
+    east = pltpu.roll(east, 1, 1)
+    north = pltpu.roll(north, 1, 0)
     surface = pressure + loading
     loading_out[...] = loading[0:rows, 0:cols]
     surface_out[...] = surface[0:rows, 0:cols]
@@ -529,6 +538,7 @@
             pltpu.VMEM((1, degrees), f32),
             pltpu.VMEM((1, wavenumbers.shape[0]), jnp.int32),
             pltpu.VMEM((4, deep, width), f32),
+            pltpu.VMEM((2, deep, width), f32),
             pltpu.VMEM((own * n_lon, LANES), f32),
             pltpu.VMEM((2 * own * n_lon, width), jnp.bfloat16),
             pltpu.VMEM((2 * own * n_lon, width), jnp.bfloat16),

time: 42.3 us -> 42.2 us (level)
  no operation moved by 1% of the time
where the time goes in v5:
time: 42.2 us; the launch traced here: 42.1 us
  Pallas kernels  41.4 us (98%)
  between operations  0.64 us (2%)
    pallas_call x1, Pallas kernels, shards(): pl.pallas_call(functools.partial(kernel, n_lat, n_lon), out_shape=(held,...  40.6 us

profile of v5, /device:TPU:1, one launch (start us, length us, event | category | flops | bytes accessed | tf_op | source)
XLA Modules:
  0.0 42.1 jit_solution(13483872033907436876)
XLA Ops:
  0.6 40.6 %shard_map.102 = (f32[64,270]{1,0:T(8,128)S(1)}, f32[64,270]{1,0:T(8,128)S(1)}, f32[64,270]{1,0:T(8,128)S(1)}, f32[64,270]{1,0:T(8,128)S(1)}) custom-call(f32[64,270]{1,0:T(8,128)} %height_hbm.1, f32[64,270]{1,0:T(8,128)} %east_hbm.1, f32[64,270]{1,0:T(8,128)} %north_hbm.1, s32[64,270]{1,0:T(8,128)} %land_hbm.1, f32[4,64,2048]{2,1,0:T(8,128)} %legendre_ref.1, ...), custom_call_target="tpu_custom_call" | custom-call | tf_op jit(solution)/shard_map/pallas_call | solution.py:528
  41.3 0.8 %shard_map.103 = (f32[64,270]{1,0:T(8,128)}, f32[64,270]{1,0:T(8,128)}, f32[64,270]{1,0:T(8,128)}, f32[64,270]{1,0:T(8,128)}) custom-call(f32[64,270]{1,0:T(8,128)S(1)} %get-tuple-element.8.a_ref, f32[64,270]{1,0:T(8,128)S(1)} %get-tuple-element.9.b_ref, f32[64,270]{1,0:T(8,128)S(1)} %get-tuple-element.10.c_ref, f32[64,270]{1,0:T(8,128)S(1)} %get-tuple-element.11.d_ref), custom_call_target="tpu_custom_call" | custom-call | tf_op jit(solution)/shard_map/pallas_call | solution.py:587

commit v6 on v5

--- a/solution.py
+++ b/solution.py
@@ -111,6 +111,8 @@
     edge_recv,
     c_send,
     c_recv,
+    d_send,
+    d_recv,
 ):
     lat = lax.axis_index("lat")
     lon = lax.axis_index("lon")
@@ -157,7 +159,19 @@
 
     count = waves_ref.shape[1]
     by_slot[...] = jnp.broadcast_to(waves_ref[...].astype(jnp.float32), (LANES, count)).T
-    waves = jnp.concatenate([by_slot[pl.ds(m, n_lon, stride=own), :] for m in range(own)], axis=0)
+    chips = n_lon // 2
+    waves = jnp.concatenate(
+        [
+            by_slot[pl.ds(own * c + m, chips, stride=2 * own), :]
+            for m in range(own)
+            for c in range(2)
+        ],
+        axis=0,
+    )
+
+    def slot_of(device):
+        return lax.rem(device, 2) * chips + lax.div(device, 2)
+
     start = jnp.bitwise_and(waves.astype(jnp.int32) * lon, n_lon - 1).astype(jnp.float32) * cols
     quarter = period // 4
     lane = lax.broadcasted_iota(jnp.int32, (16, width), 1)
@@ -232,8 +246,8 @@
         pltpu.make_async_copy(ref.at[pl.ds(0, n)], ref.at[pl.ds(0, n)], send_sem.at[k]).wait()
 
     for _, other in lons:
-        lon_copy(0, a_out.at[other], a_in.at[lon], other).start()
-    a_in[lon] = a_out[lon]
+        lon_copy(0, a_out.at[slot_of(other)], a_in.at[lon], other).start()
+    a_in[lon] = a_out[slot_of(lon)]
 
     below, above = jnp.minimum(lat + 1, n_lat - 1), jnp.maximum(lat - 1, 0)
 
@@ -428,9 +442,42 @@
     rim = jnp.sum(rim, axis=0, keepdims=True)
     packet = jnp.where(row8 < 4, body, rim) * (1.0 / math.sqrt(count))
     d_out[...] = packet[0:5]
-    for _, other in lons:
-        lon_copy(3, d_out, d_in.at[lon], other).start()
-    d_in[lon] = d_out[...]
+    n_z = n_lon // 4
+    z, x_lo, core = lax.div(lon, 4), lax.rem(lax.div(lon, 2), 2), lax.rem(lon, 2)
+    mine = slot_of(lon)
+
+    def packet_copy(src, slots, k, other):
+        return pltpu.make_async_remote_copy(
+            src_ref=src,
+            dst_ref=d_in.at[slots],
+            send_sem=d_send.at[k],
+            recv_sem=d_recv.at[k],
+            device_id=(lat, other),
+            device_id_type=MESH,
+        )
+
+    def packets(count):
+        return d_in.at[pl.ds(0, count)]
+
+    far = n_z // 2
+    near = sorted((dz for dz in range(n_z) if dz != far), key=lambda dz: hops(n_z, dz))
+    for dx, dc in ((1, 1), (1, 0), (0, 1), (0, 0)):
+        other = lax.rem(z + far, n_z) * 4
+        other = other + (1 - x_lo if dx else x_lo) * 2 + (1 - core if dc else core)
+        packet_copy(d_out, mine, far, other).start()
+    for dz in near[::-1]:
+        for dx in (1, 0):
+            if dz or dx:
+                other = lax.rem(z + dz, n_z) * 4 + (1 - x_lo if dx else x_lo) * 2 + core
+                pltpu.make_async_remote_copy(
+                    src_ref=d_out,
+                    dst_ref=d_in.at[mine],
+                    send_sem=d_send.at[far],
+                    recv_sem=d_recv.at[(n_z - dz) % n_z],
+                    device_id=(lat, other),
+                    device_id_type=MESH,
+                ).start()
+    d_in[mine] = d_out[...]
 
     wide, tall = width - 1, deep - 1
     wet = fields[3]
@@ -440,7 +487,15 @@
     fields[3] = step
     steps[0] = pltpu.roll(step, wide, 1)
     steps[1] = pltpu.roll(step, tall, 0)
-    all_received(3, d_in, n_lon - 1)
+
+    for dz in near:
+        count_in = 2 if dz else 1
+        pltpu.make_async_copy(packets(count_in), packets(count_in), d_recv.at[dz]).wait()
+        pair = pl.ds(core * chips + 2 * lax.rem(z + dz, n_z), 2)
+        packet_copy(d_in.at[pair], pair, n_z, lon + 1 - 2 * core).start()
+    handed = 2 * len(near)
+    pltpu.make_async_copy(packets(handed), packets(handed), d_recv.at[n_z]).wait()
+    pltpu.make_async_copy(packets(4), packets(4), d_recv.at[far]).wait()
 
     rows_kt = jnp.concatenate([d_in[:, m, :] for m in range(own)], axis=0)
     rows_tk = rows_kt.T
@@ -492,7 +547,8 @@
     all_sent(1, b_in, n_lat - 1)
     for copy in c_copies:
         copy.wait_send()
-    all_sent(3, d_in, n_lon - 1)
+    pltpu.make_async_copy(packets(handed), packets(handed), d_send.at[n_z]).wait()
+    pltpu.make_async_copy(packets(handed + 3), packets(handed + 3), d_send.at[far]).wait()
     left_copy.wait_send()
     right_copy.wait_send()
 
@@ -559,12 +615,14 @@
             pltpu.VMEM((deep, LANES), f32),
             pltpu.VMEM((deep, LANES), f32),
             pltpu.SemaphoreType.DMA((7,)),
-            pltpu.SemaphoreType.DMA((4,)),
-            pltpu.SemaphoreType.DMA((4,)),
+            pltpu.SemaphoreType.DMA((2,)),
+            pltpu.SemaphoreType.DMA((2,)),
             pltpu.SemaphoreType.DMA((6,)),
             pltpu.SemaphoreType.DMA((6,)),
             pltpu.SemaphoreType.DMA((n_lat // 2,)),
             pltpu.SemaphoreType.DMA((n_lat // 2,)),
+            pltpu.SemaphoreType.DMA((n_lon // 4 + 1,)),
+            pltpu.SemaphoreType.DMA((n_lon // 4 + 1,)),
         ],
         compiler_params=pltpu.CompilerParams(
             collective_id=0, has_side_effects=True, vmem_limit_bytes=24 << 20

time: 42.2 us -> 43.3 us (1.026)
  Pallas kernels: 41.4 us -> 42.5 us
    pallas_call x1, Pallas kernels: 40.6 us -> 41.8 us  [shards(): pl.pallas_call(functools.partial(kernel, n_lat, n_lon), out_shape=(held,...]
where the time goes in v6:
time: 43.3 us; the launch traced here: 43.2 us
  Pallas kernels  42.5 us (98%)
  between operations  0.64 us (1%)
    pallas_call x1, Pallas kernels, shards(): pl.pallas_call(functools.partial(kernel, n_lat, n_lon), out_shape=(held,...  41.8 us

profile of v6, /device:TPU:1, one launch (start us, length us, event | category | flops | bytes accessed | tf_op | source)
XLA Modules:
  0.0 43.2 jit_solution(15176757115503446240)
XLA Ops:
  0.6 41.8 %shard_map.102 = (f32[64,270]{1,0:T(8,128)S(1)}, f32[64,270]{1,0:T(8,128)S(1)}, f32[64,270]{1,0:T(8,128)S(1)}, f32[64,270]{1,0:T(8,128)S(1)}) custom-call(f32[64,270]{1,0:T(8,128)} %height_hbm.1, f32[64,270]{1,0:T(8,128)} %east_hbm.1, f32[64,270]{1,0:T(8,128)} %north_hbm.1, s32[64,270]{1,0:T(8,128)} %land_hbm.1, f32[4,64,2048]{2,1,0:T(8,128)} %legendre_ref.1, ...), custom_call_target="tpu_custom_call" | custom-call | tf_op jit(solution)/shard_map/pallas_call | solution.py:584
  42.4 0.8 %shard_map.103 = (f32[64,270]{1,0:T(8,128)}, f32[64,270]{1,0:T(8,128)}, f32[64,270]{1,0:T(8,128)}, f32[64,270]{1,0:T(8,128)}) custom-call(f32[64,270]{1,0:T(8,128)S(1)} %get-tuple-element.8.a_ref, f32[64,270]{1,0:T(8,128)S(1)} %get-tuple-element.9.b_ref, f32[64,270]{1,0:T(8,128)S(1)} %get-tuple-element.10.c_ref, f32[64,270]{1,0:T(8,128)S(1)} %get-tuple-element.11.d_ref), custom_call_target="tpu_custom_call" | custom-call | tf_op jit(solution)/shard_map/pallas_call | solution.py:645

commit v7 on v5

--- a/solution.py
+++ b/solution.py
@@ -256,25 +256,35 @@
         fields.at[:, rows + HALO : rows + 2 * HALO, :],
         (below, lon),
     )
-    low_leg = edge_copy(
-        2, legendre_ref.at[:, 0:HALO, :], leg_halo.at[:, 0:HALO, :], (above, lon)
-    )
-    high_leg = edge_copy(
-        3,
-        legendre_ref.at[:, rows - HALO : rows, :],
-        leg_halo.at[:, HALO : 2 * HALO, :],
-        (below, lon),
-    )
+    halves = [pl.ds(0, own // 2), pl.ds(own // 2, own - own // 2)]
+    low_leg = [
+        edge_copy(
+            k,
+            legendre_ref.at[some, 0:HALO, :],
+            leg_halo.at[some, 0:HALO, :],
+            (above, lon),
+        )
+        for k, some in zip((2, 6), halves)
+    ]
+    high_leg = [
+        edge_copy(
+            k,
+            legendre_ref.at[some, rows - HALO : rows, :],
+            leg_halo.at[some, HALO : 2 * HALO, :],
+            (below, lon),
+        )
+        for k, some in zip((3, 7), halves)
+    ]
 
     @pl.when(lat > 0)
     def _():
         low_rows.start()
-        low_leg.start()
+        low_leg[0].start()
 
     @pl.when(lat < n_lat - 1)
     def _():
         high_rows.start()
-        high_leg.start()
+        high_leg[0].start()
 
     @pl.when(lat == 0)
     def _():
@@ -322,6 +332,14 @@
 
     @pl.when(lat > 0)
     def _():
+        low_leg[1].start()
+
+    @pl.when(lat < n_lat - 1)
+    def _():
+        high_leg[1].start()
+
+    @pl.when(lat > 0)
+    def _():
         high_rows.wait_recv()
 
     @pl.when(lat < n_lat - 1)
@@ -393,11 +411,13 @@
 
     @pl.when(lat > 0)
     def _():
-        high_leg.wait_recv()
+        for copy in high_leg:
+            copy.wait_recv()
 
     @pl.when(lat < n_lat - 1)
     def _():
-        low_leg.wait_recv()
+        for copy in low_leg:
+            copy.wait_recv()
 
     both_leg = split(leg_halo[...].reshape(own * 2 * HALO, degrees))
     leg_high[inner_rows:, :], leg_low[inner_rows:, :] = both_leg
@@ -498,11 +518,13 @@
 
     @pl.when(lat > 0)
     def _():
-        low_leg.wait_send()
+        for copy in low_leg:
+            copy.wait_send()
 
     @pl.when(lat < n_lat - 1)
     def _():
-        high_leg.wait_send()
+        for copy in high_leg:
+            copy.wait_send()
 
 
 def write_kernel(a_ref, b_ref, c_ref, d_ref, a_out, b_out, c_out, d_out, sem):
@@ -561,8 +583,8 @@
             pltpu.SemaphoreType.DMA((7,)),
             pltpu.SemaphoreType.DMA((4,)),
             pltpu.SemaphoreType.DMA((4,)),
-            pltpu.SemaphoreType.DMA((6,)),
-            pltpu.SemaphoreType.DMA((6,)),
+            pltpu.SemaphoreType.DMA((8,)),
+            pltpu.SemaphoreType.DMA((8,)),
             pltpu.SemaphoreType.DMA((n_lat // 2,)),
             pltpu.SemaphoreType.DMA((n_lat // 2,)),
         ],

time: 42.2 us -> 40.9 us (0.969)
  Pallas kernels: 41.4 us -> 40.1 us
    pallas_call x1, Pallas kernels: 40.6 us -> 39.4 us  [shards(): pl.pallas_call(functools.partial(kernel, n_lat, n_lon), out_shape=(held,...]
where the time goes in v7:
time: 40.9 us; the launch traced here: 40.8 us
  Pallas kernels  40.1 us (98%)
  between operations  0.64 us (2%)
    pallas_call x1, Pallas kernels, shards(): pl.pallas_call(functools.partial(kernel, n_lat, n_lon), out_shape=(held,...  39.4 us

profile of v7, /device:TPU:1, one launch (start us, length us, event | category | flops | bytes accessed | tf_op | source)
XLA Modules:
  0.0 40.8 jit_solution(6768269829099005510)
XLA Ops:
  0.6 39.4 %shard_map.102 = (f32[64,270]{1,0:T(8,128)S(1)}, f32[64,270]{1,0:T(8,128)S(1)}, f32[64,270]{1,0:T(8,128)S(1)}, f32[64,270]{1,0:T(8,128)S(1)}) custom-call(f32[64,270]{1,0:T(8,128)} %height_hbm.1, f32[64,270]{1,0:T(8,128)} %east_hbm.1, f32[64,270]{1,0:T(8,128)} %north_hbm.1, s32[64,270]{1,0:T(8,128)} %land_hbm.1, f32[4,64,2048]{2,1,0:T(8,128)} %legendre_ref.1, ...), custom_call_target="tpu_custom_call" | custom-call | tf_op jit(solution)/shard_map/pallas_call | solution.py:550
  40.0 0.8 %shard_map.103 = (f32[64,270]{1,0:T(8,128)}, f32[64,270]{1,0:T(8,128)}, f32[64,270]{1,0:T(8,128)}, f32[64,270]{1,0:T(8,128)}) custom-call(f32[64,270]{1,0:T(8,128)S(1)} %get-tuple-element.8.a_ref, f32[64,270]{1,0:T(8,128)S(1)} %get-tuple-element.9.b_ref, f32[64,270]{1,0:T(8,128)S(1)} %get-tuple-element.10.c_ref, f32[64,270]{1,0:T(8,128)S(1)} %get-tuple-element.11.d_ref), custom_call_target="tpu_custom_call" | custom-call | tf_op jit(solution)/shard_map/pallas_call | solution.py:609

commit v8 on v7

--- a/solution.py
+++ b/solution.py
@@ -256,7 +256,7 @@
         fields.at[:, rows + HALO : rows + 2 * HALO, :],
         (below, lon),
     )
-    halves = [pl.ds(0, own // 2), pl.ds(own // 2, own - own // 2)]
+    halves = [pl.ds(0, own // 4), pl.ds(own // 4, own - own // 4)]
     low_leg = [
         edge_copy(
             k,

time: 40.9 us -> 41.2 us (level)
  no operation moved by 1% of the time
where the time goes in v8:
time: 41.2 us; the launch traced here: 41 us
  Pallas kernels  40.4 us (98%)
  between operations  0.64 us (2%)
    pallas_call x1, Pallas kernels, shards(): pl.pallas_call(functools.partial(kernel, n_lat, n_lon), out_shape=(held,...  39.6 us

profile of v8, /device:TPU:1, one launch (start us, length us, event | category | flops | bytes accessed | tf_op | source)
XLA Modules:
  0.0 41.0 jit_solution(2641104840356965288)
XLA Ops:
  0.6 39.6 %shard_map.102 = (f32[64,270]{1,0:T(8,128)S(1)}, f32[64,270]{1,0:T(8,128)S(1)}, f32[64,270]{1,0:T(8,128)S(1)}, f32[64,270]{1,0:T(8,128)S(1)}) custom-call(f32[64,270]{1,0:T(8,128)} %height_hbm.1, f32[64,270]{1,0:T(8,128)} %east_hbm.1, f32[64,270]{1,0:T(8,128)} %north_hbm.1, s32[64,270]{1,0:T(8,128)} %land_hbm.1, f32[4,64,2048]{2,1,0:T(8,128)} %legendre_ref.1, ...), custom_call_target="tpu_custom_call" | custom-call | tf_op jit(solution)/shard_map/pallas_call | solution.py:550
  40.3 0.8 %shard_map.103 = (f32[64,270]{1,0:T(8,128)}, f32[64,270]{1,0:T(8,128)}, f32[64,270]{1,0:T(8,128)}, f32[64,270]{1,0:T(8,128)}) custom-call(f32[64,270]{1,0:T(8,128)S(1)} %get-tuple-element.8.a_ref, f32[64,270]{1,0:T(8,128)S(1)} %get-tuple-element.9.b_ref, f32[64,270]{1,0:T(8,128)S(1)} %get-tuple-element.10.c_ref, f32[64,270]{1,0:T(8,128)S(1)} %get-tuple-element.11.d_ref), custom_call_target="tpu_custom_call" | custom-call | tf_op jit(solution)/shard_map/pallas_call | solution.py:609
